TPU v7x, 256 devices: a whole 4x4x8 slice. The times are simulated.
256 devices in a mesh: aux: 16 (over z, core), pairs: 16 (over x, y).
Axes of the slice: x: 4, y: 4, z: 8, core: 2. Of those that a mesh axis runs over, the one named last changes fastest.
Arguments:
- amplitudes: bfloat16 [32, 256, 256], P(None, 'aux', 'pairs'), may hold values from -6 to 6
- three_index: bfloat16 [448, 256, 256], P('aux'), may hold values from -0.078125 to 0.078125
- virt_energy: float32 [256], replicated, may hold values from 0.2 to 1.5
- pair_energy: float32 [32], replicated, may hold values from -1.5 to -0.3
- owner: int32 [32], replicated, may hold values from 0 to 15, as said below
- partner: int32 [32], replicated, may hold values from 0 to 31, as said below
Outputs:
- blocks: float32 [64, 256, 256], P('pairs', 'aux')
Inputs may be any that keep to these rules, and one draw needn't show every extreme that they name: `owner`: no group index is named by more than 4 pairs, and one group is named by exactly 4 pairs. partner[partner[p]] == p for every pair p.
All inputs are finite; a program needn't handle non-finite values.
Results may differ from a plain program's by a relative error of at most 0.0029.
Values may be sent and summed in bfloat16 or wider, within the bound.
No kernel may reach another device: no remote copies, remote signals or barrier semaphores. Data moves between devices by JAX's collectives and lax.ppermute only.
A program may use at most 64 MiB of HBM per device.

v0:
```python
import jax
import jax.numpy as jnp
from jax import lax
from jax.sharding import PartitionSpec as P


def ladder_rows(amp_tiles, three_index):
    whole_tiles = lax.all_gather(amp_tiles, "aux", axis=1, tiled=True)

    def one_slot(slot_tile):
        half_product = jnp.einsum(
            "cd,qbd->qcb", slot_tile, three_index, preferred_element_type=jnp.float32
        ).astype(jnp.bfloat16)
        return jnp.einsum(
            "qac,qcb->ab", three_index, half_product, preferred_element_type=jnp.float32
        )

    running = lax.map(one_slot, whole_tiles)
    return lax.psum_scatter(running, "aux", scatter_dimension=1, tiled=True)


def scale_turn(summed, energies, virt_energy, row_count):
    row_offset = lax.axis_index("aux") * row_count
    virt_rows = lax.dynamic_slice_in_dim(virt_energy, row_offset, row_count)
    divisor = virt_rows[None, :, None] + virt_energy[None, None, :] - energies[:, None, None]
    scaled = summed / divisor
    turned = lax.all_to_all(scaled, "aux", split_axis=2, concat_axis=1, tiled=True)
    return (scaled, jnp.swapaxes(turned, 1, 2))


def per_device(amplitudes, three_index, virt_energy, pair_energy, owner, partner):
    groups = lax.axis_size("pairs")
    my_group = lax.axis_index("pairs")
    pairs_all = owner.shape[0]
    row_count = amplitudes.shape[1]
    virt_count = three_index.shape[1]
    per_group = pairs_all // groups
    capacity = 2 * per_group
    pair_ids = jnp.arange(pairs_all, dtype=jnp.int32)
    earlier = (owner[None, :] == owner[:, None]) & (pair_ids[None, :] < pair_ids[:, None])
    position = owner * capacity + jnp.sum(earlier.astype(jnp.int32), axis=1)
    partner_table = partner[:, None] == pair_ids[None, :]
    own_ids = my_group * capacity + jnp.arange(capacity, dtype=jnp.int32)
    own_link = (position[None, :] == own_ids[:, None]).astype(jnp.float32)
    slot_ids = jnp.arange(groups * capacity, dtype=jnp.int32)
    slot_pick = position[None, :] == slot_ids[:, None]
    outgoing = jnp.einsum(
        "sp,prc->src",
        slot_pick.astype(jnp.bfloat16),
        amplitudes,
        preferred_element_type=jnp.float32,
    ).astype(jnp.bfloat16)
    outgoing = outgoing.reshape(groups, capacity, row_count, amplitudes.shape[2])
    arrived = lax.all_to_all(outgoing, "pairs", split_axis=0, concat_axis=3, tiled=True).reshape(
        capacity, row_count, virt_count
    )
    summed = ladder_rows(arrived, three_index)
    energies = jnp.dot(own_link, pair_energy, precision=lax.Precision.HIGHEST)
    scaled, flipped = scale_turn(summed, energies, virt_energy, row_count)
    partner_pos = jnp.sum(jnp.where(partner_table, position[None, :], 0), axis=1)
    partner_link = jnp.dot(
        own_link,
        (partner_pos[:, None] == slot_ids[None, :]).astype(jnp.float32),
        precision=lax.Precision.HIGHEST,
    )
    partner_part = jnp.einsum(
        "st,trb->srb",
        partner_link,
        lax.all_gather(flipped, "pairs", axis=0, tiled=True),
        precision=lax.Precision.HIGHEST,
    )
    return scaled + partner_part


def solution(mesh):
    placed = (P(None, "aux", "pairs"), P("aux", None, None), P(), P(), P(), P())
    return jax.shard_map(
        per_device, mesh=mesh, in_specs=placed, out_specs=P("pairs", "aux", None), check_vma=False
    )
```

profile of v0, /device:TPU:1, one launch (start us, length us, event | category | flops | bytes accessed | tf_op | source)
XLA Modules:
  0.0 273.9 jit_solution(17575334339474999060)
XLA Ops:
  6.5 0.9 convert_reduce_fusion
  7.4 0.7 multiply_add_fusion
  8.6 0.9 reshape.59
  9.5 7.6 %all-to-all-start = ((bf16[16,2,512]{2,1,0:T(2,128)(2,1)}), bf16[16,2,512]{2,1,0:T(2,128)(2,1)S(1)}, u32[]{:S(2)}, u32[]{:S(2)}) async-start(bf16[16,2,512]{2,1,0:T(2,128)(2,1)} %reshape.59), calls=%async_computation | async-start | bytes 65536 | tf_op jit(solution)/shard_map/all_to_all | solution.py:54
  17.1 6.4 %all-to-all-done = bf16[16,2,512]{2,1,0:T(2,128)(2,1)S(1)} async-done(((bf16[16,2,512]{2,1,0:T(2,128)(2,1)}), bf16[16,2,512]{2,1,0:T(2,128)(2,1)S(1)}, u32[]{:S(2)}, u32[]{:S(2)}) %all-to-all-start) | async-done | bytes 32800 | tf_op jit(solution)/shard_map/all_to_all | solution.py:54
  24.2 23.4 %all_gather.6 = bf16[4,256,256]{2,1,0:T(8,128)(2,1)S(1)} all-gather(bf16[4,16,256]{2,1,0:T(8,128)(2,1)S(1)} %reshape.50), channel_id=1, replica_groups=mesh['aux'=16,'pairs'=16] {'aux'}, dimensions={1}, use_global_device_ids=true | all-gather | bytes 557056 | tf_op jit(solution)/shard_map/all_gather | solution.py:8
  47.6 49.3 %while.10 = (s32[]{:T(128)}, f32[4,256,256]{2,0,1:T(4,128)}, bf16[4,256,256]{2,1,0:T(8,128)(2,1)S(1)}, bf16[28,256,256]{2,1,0:T(8,128)(2,1)}, s32[]{:T(128)}, /*index=5*/s32[]{:T(128)}) while((s32[]{:T(128)}, f32[4,256,256]{2,0,1:T(4,128)}, bf16[4,256,256]{2,1,0:T(8,128)(2,1)S(1)}, bf16[28,256,256]{2,1,0:T(8,128)(2,1)}, s32[]{:T(128)}, ...), condition=%wide.region_2.3_spmd, body=%wide.region_1.2_spmd.sunk | while | flops 1880883200 | bytes 8781909 | solution.py:18
  47.6 5.5 %fusion.39 = f32[1,256,256]{1,2,0:T(8,128)S(1)} fusion(bf16[28,256,256]{2,1,0:T(8,128)(2,1)} %get-tuple-element.76, bf16[4,256,256]{2,1,0:T(8,128)(2,1)S(1)} %get-tuple-element.75, s32[]{:T(128)S(6)} %copy.55), kind=kOutput, calls=%fused_computation.4.clone.1 | convolution fusion | flops 1880883200 | bytes 7733252 | tf_op jit(solution)/shard_map/while/body/eval_jaxpr/qac,qcb->ab/dot_general | solution.py:14
  53.2 6.7 %dynamic_update_slice.5 = f32[4,256,256]{2,0,1:T(4,128)} dynamic-update-slice(f32[4,256,256]{2,0,1:T(4,128)} %get-tuple-element.68, f32[1,256,256]{2,0,1:T(1,128)S(1)} %copy.51, s32[]{:T(128)S(6)} %copy.55, s32[]{:T(128)} %constant.7.clone.1..sunk, s32[]{:T(128)} %constant.7.clone.1..sunk) | dynamic-update-slice | bytes 524292 | tf_op jit(solution)/shard_map/while/body/jit(dynamic_update_index_in_dim)/dynamic_update_slice | solution.py:18
  59.9 5.5 %fusion.39 = f32[1,256,256]{1,2,0:T(8,128)S(1)} fusion(bf16[28,256,256]{2,1,0:T(8,128)(2,1)} %get-tuple-element.76, bf16[4,256,256]{2,1,0:T(8,128)(2,1)S(1)} %get-tuple-element.75, s32[]{:T(128)S(6)} %copy.55), kind=kOutput, calls=%fused_computation.4.clone.1 | convolution fusion | flops 1880883200 | bytes 7733252 | tf_op jit(solution)/shard_map/while/body/eval_jaxpr/qac,qcb->ab/dot_general | solution.py:14
  65.6 6.7 %dynamic_update_slice.5 = f32[4,256,256]{2,0,1:T(4,128)} dynamic-update-slice(f32[4,256,256]{2,0,1:T(4,128)} %get-tuple-element.68, f32[1,256,256]{2,0,1:T(1,128)S(1)} %copy.51, s32[]{:T(128)S(6)} %copy.55, s32[]{:T(128)} %constant.7.clone.1..sunk, s32[]{:T(128)} %constant.7.clone.1..sunk) | dynamic-update-slice | bytes 524292 | tf_op jit(solution)/shard_map/while/body/jit(dynamic_update_index_in_dim)/dynamic_update_slice | solution.py:18
  72.2 5.5 %fusion.39 = f32[1,256,256]{1,2,0:T(8,128)S(1)} fusion(bf16[28,256,256]{2,1,0:T(8,128)(2,1)} %get-tuple-element.76, bf16[4,256,256]{2,1,0:T(8,128)(2,1)S(1)} %get-tuple-element.75, s32[]{:T(128)S(6)} %copy.55), kind=kOutput, calls=%fused_computation.4.clone.1 | convolution fusion | flops 1880883200 | bytes 7733252 | tf_op jit(solution)/shard_map/while/body/eval_jaxpr/qac,qcb->ab/dot_general | solution.py:14
  77.9 6.7 %dynamic_update_slice.5 = f32[4,256,256]{2,0,1:T(4,128)} dynamic-update-slice(f32[4,256,256]{2,0,1:T(4,128)} %get-tuple-element.68, f32[1,256,256]{2,0,1:T(1,128)S(1)} %copy.51, s32[]{:T(128)S(6)} %copy.55, s32[]{:T(128)} %constant.7.clone.1..sunk, s32[]{:T(128)} %constant.7.clone.1..sunk) | dynamic-update-slice | bytes 524292 | tf_op jit(solution)/shard_map/while/body/jit(dynamic_update_index_in_dim)/dynamic_update_slice | solution.py:18
  84.6 5.5 %fusion.39 = f32[1,256,256]{1,2,0:T(8,128)S(1)} fusion(bf16[28,256,256]{2,1,0:T(8,128)(2,1)} %get-tuple-element.76, bf16[4,256,256]{2,1,0:T(8,128)(2,1)S(1)} %get-tuple-element.75, s32[]{:T(128)S(6)} %copy.55), kind=kOutput, calls=%fused_computation.4.clone.1 | convolution fusion | flops 1880883200 | bytes 7733252 | tf_op jit(solution)/shard_map/while/body/eval_jaxpr/qac,qcb->ab/dot_general | solution.py:14
  90.2 6.7 %dynamic_update_slice.5 = f32[4,256,256]{2,0,1:T(4,128)} dynamic-update-slice(f32[4,256,256]{2,0,1:T(4,128)} %get-tuple-element.68, f32[1,256,256]{2,0,1:T(1,128)S(1)} %copy.51, s32[]{:T(128)S(6)} %copy.55, s32[]{:T(128)} %constant.7.clone.1..sunk, s32[]{:T(128)} %constant.7.clone.1..sunk) | dynamic-update-slice | bytes 524292 | tf_op jit(solution)/shard_map/while/body/jit(dynamic_update_index_in_dim)/dynamic_update_slice | solution.py:18
  97.0 0.6 dynamic-slice
  98.6 104.5 %all-reduce.3.cloned.1.call-done = f32[4,256,256]{2,0,1:T(4,128)} async-done(((f32[4,256,256]{2,0,1:T(4,128)}), f32[4,256,256]{2,0,1:T(4,128)}) %all-reduce.3.cloned.1.call-update) | async-done | bytes 1048592
  203.1 0.9 dynamic-slice_divide_fusion
  204.7 14.4 %all_to_all.33 = f32[16,1,1024]{2,1,0:T(1,128)S(1)} all-to-all(f32[16,1,1024]{2,1,0:T(1,128)S(1)} %reshape.61), channel_id=1, replica_groups=mesh['aux'=16,'pairs'=16] {'aux'}, dimensions={0} | all-to-all | bytes 131072 | tf_op jit(solution)/shard_map/all_to_all | solution.py:27
  219.6 0.8 reduce
  221.1 0.9 all_to_all.30
  222.4 41.7 %all-gather.2.cloned.1.call-done = f32[64,16,256]{2,1,0:T(8,128)} async-done(((f32[4,16,256]{2,1,0:T(8,128)}), f32[64,16,256]{2,1,0:T(8,128)}) %all-gather.2.cloned.1.call-update) | async-done | bytes 1048592 | tf_op jit(solution)/shard_map/all_gather | solution.py:69
  264.1 2.4 convolution_add_fusion
  266.4 0.6 copy.44
  (36 shorter events, 4.5 us)
Async XLA Ops:
  6.5 1.6 copy-start
  9.5 14.1 %all-to-all-start = ((bf16[16,2,512]{2,1,0:T(2,128)(2,1)}), bf16[16,2,512]{2,1,0:T(2,128)(2,1)S(1)}, u32[]{:S(2)}, u32[]{:S(2)}) async-start(bf16[16,2,512]{2,1,0:T(2,128)(2,1)} %reshape.59), calls=%async_computation | async-start | bytes 65536 | tf_op jit(solution)/shard_map/all_to_all | solution.py:54
  17.1 186.0 %all-reduce.3.cloned.1.call-start = ((), (), s32[]{:S(2)}) async-start(), calls=%async_computation.3 | async-start | bytes 2097152
  47.6 49.4 %copy-start.4 = (u32[256]{0:T(256)S(1)}, u32[256]{0:T(256)}, u32[]{:S(2)}) copy-start(u32[256]{0:T(256)} %constant.30) | copy-start | bytes 3076
  47.6 50.7 %copy-start.1 = (f32[256]{0:T(256)S(1)}, f32[256]{0:T(256)}, u32[]{:S(2)}) copy-start(f32[256]{0:T(256)} %param.10) | copy-start | bytes 3076
  47.6 50.7 %copy-start.2 = (f32[32]{0:T(128)S(1)}, f32[32]{0:T(128)}, u32[]{:S(2)}) copy-start(f32[32]{0:T(128)} %param.11) | copy-start | bytes 388
  96.9 125.1 %copy-start.3 = (s32[32]{0:T(128)S(1)}, s32[32]{0:T(128)}, u32[]{:S(2)}) copy-start(s32[32]{0:T(128)} %param.13) | copy-start | bytes 388
  96.9 167.1 %all-gather.2.cloned.1.call-start = ((), (), s32[]{:S(2)}) async-start(), calls=%async_computation.2 | async-start | bytes 1114112 | tf_op jit(solution)/shard_map/all_gather | solution.py:69
Sparse Core Ops, SparseCore 0:
  97.0 105.9 all-reduce.2
  222.1 41.8 all-gather.1
where the time goes:
time: 275 us; the launch traced here: 274 us
  waiting for transfers between devices  153 us (56%)
  blocking collectives  37.8 us (14%)
  local copies, waits for them, and re-layouts  33.2 us (12%)
  matrix products  24.8 us (9%)
  between operations  14.2 us (5%)
  starting transfers between devices  7.66 us (3%)
  other arithmetic  3.58 us (1%)
    unnamed x3, waiting for transfers between devices  105 us
    all_gather x1, waiting for transfers between devices, per_device(): lax.all_gather(flipped, 'pairs', axis=0, tiled=True)  41.7 us
    dynamic_update_slice x8, local copies, waits for them, and re-layouts, ladder_rows(): running = lax.map(one_slot, whole_tiles)  27.4 us
    all_gather x1, blocking collectives, ladder_rows(): whole_tiles = lax.all_gather(amp_tiles, 'aux', axis=1, tiled=True)  23.4 us
    dot_general x4, matrix products, one_slot(): jnp.einsum('qac,qcb->ab', three_index, half_product, preferred_element_ty...  21.9 us
    all_to_all x1, blocking collectives, scale_turn(): lax.all_to_all(scaled, 'aux', split_axis=2, concat_axis=1, tiled=True)  14.4 us
    all_to_all x1, starting transfers between devices, per_device(): lax.all_to_all(outgoing, 'pairs', split_axis=0, concat_axis=3, tiled=True)  7.57 us
    all_to_all x1, waiting for transfers between devices, per_device(): lax.all_to_all(outgoing, 'pairs', split_axis=0, concat_axis=3, tiled=True)  6.41 us
  transfers between devices with their start and end apart: 3, of which 3 were waited for; matrix products, arithmetic and copies ran while one was open for 0% of the time, Pallas kernels for 0%

commit v1 on v0

v1 whole, which is shorter than its diff:
```python
import jax
import jax.numpy as jnp
from jax import lax
from jax.experimental import pallas as pl
from jax.experimental.pallas import tpu as pltpu
from jax.sharding import PartitionSpec as P


def ladder_kernel(same_ref, pair_e_ref, amp_ref, b_ref, row_e_ref, col_e_ref, out_ref, amp_t, acc):
    step = pl.program_id(0)
    virt = b_ref.shape[1]
    count = b_ref.shape[0]

    @pl.when(step == 0)
    def _():
        for s in range(2):
            amp_t[:, s * virt : (s + 1) * virt] = amp_ref[s].T
        acc[...] = jnp.zeros_like(acc)

    rows = b_ref[...].reshape(count * virt, virt)
    half = jnp.dot(rows, amp_t[...], preferred_element_type=jnp.float32).astype(jnp.bfloat16)
    for s in range(2):
        total = acc[s]
        for k in range(count):
            total += lax.dot_general(
                half[k * virt : (k + 1) * virt, s * virt : (s + 1) * virt],
                b_ref[k],
                (((1,), (1,)), ((), ())),
                preferred_element_type=jnp.float32,
            )
        acc[s] = total

    @pl.when(step == pl.num_programs(0) - 1)
    def _():
        sums = row_e_ref[...] + col_e_ref[...]
        first = acc[0] / (sums - pair_e_ref[0])
        second = acc[1] / (sums - pair_e_ref[1])
        same = same_ref[0] > 0
        first_n = first.T
        second_n = second.T
        blocks = (
            first_n + jnp.where(same, first, second),
            second_n + jnp.where(same, second, first),
        )
        for s in range(2):
            out_ref[:, s] = blocks[s].astype(jnp.bfloat16).reshape(out_ref.shape[0], out_ref.shape[2], virt)


def ladder(same, pair_e, amp, three_index, virt_energy, aux):
    naux, virt, _ = three_index.shape
    count = 4
    smem = pl.BlockSpec(memory_space=pltpu.SMEM)
    return pl.pallas_call(
        ladder_kernel,
        grid=(naux // count,),
        in_specs=[
            smem,
            smem,
            pl.BlockSpec((2, virt, virt), lambda i: (0, 0, 0)),
            pl.BlockSpec((count, virt, virt), lambda i: (i, 0, 0)),
            pl.BlockSpec((virt, 1), lambda i: (0, 0)),
            pl.BlockSpec((1, virt), lambda i: (0, 0)),
        ],
        out_specs=pl.BlockSpec((aux, 2, virt // aux, virt), lambda i: (0, 0, 0, 0)),
        out_shape=jax.ShapeDtypeStruct((aux, 2, virt // aux, virt), jnp.bfloat16),
        scratch_shapes=[
            pltpu.VMEM((virt, 2 * virt), jnp.bfloat16),
            pltpu.VMEM((2, virt, virt), jnp.float32),
        ],
        name="ladder",
    )(same, pair_e, amp, three_index, virt_energy[:, None], virt_energy[None, :])


def per_device(amplitudes, three_index, virt_energy, pair_energy, owner, partner):
    aux = lax.axis_size("aux")
    groups = lax.axis_size("pairs")
    my_group = lax.axis_index("pairs")
    pairs_all = owner.shape[0]
    rows, cols = amplitudes.shape[1:]
    virt = three_index.shape[1]
    capacity = 2 * (pairs_all // groups)
    ids = jnp.arange(pairs_all, dtype=jnp.int32)
    before = ids[None, :] < ids[:, None]
    leads = partner > ids
    fixed = partner == ids
    low = jnp.minimum(ids, partner)
    lead_rank = jnp.sum((leads[None, :] & (ids[None, :] < low[:, None])).astype(jnp.int32), axis=1)
    fixed_rank = jnp.sum((fixed[None, :] & before).astype(jnp.int32), axis=1)
    leaders = jnp.sum(leads.astype(jnp.int32))
    place = jnp.where(fixed, 2 * leaders + fixed_rank, 2 * lead_rank + (ids > partner))
    pick = place[None, :] == ids[:, None]
    outgoing = jnp.dot(
        pick.astype(jnp.bfloat16),
        amplitudes.reshape(pairs_all, rows * cols),
        preferred_element_type=jnp.float32,
    ).astype(jnp.bfloat16)
    outgoing = jnp.broadcast_to(
        outgoing.reshape(1, groups, 2, rows * cols), (aux, groups, 2, rows * cols)
    ).reshape(aux * groups, 2, rows * cols)
    arrived = lax.all_to_all(outgoing, ("aux", "pairs"), split_axis=0, concat_axis=0, tiled=True)
    amp = arrived.reshape(aux, groups, 2, rows, cols).transpose(2, 0, 3, 1, 4).reshape(2, virt, virt)
    mine = pick & (ids[:, None] // 2 == my_group)
    pair_e = jnp.sum(jnp.where(mine, pair_energy[None, :], 0.0), axis=1).reshape(groups, 2).sum(axis=0)
    same = (my_group >= leaders).astype(jnp.int32).reshape(1)
    partial = ladder(same, pair_e, amp, three_index, virt_energy, aux)
    shares = lax.all_to_all(partial, "aux", split_axis=0, concat_axis=0, tiled=True)
    done = jnp.sum(shares.astype(jnp.float32), axis=0).astype(jnp.bfloat16)
    spread = jnp.broadcast_to(done[None], (groups,) + done.shape)
    found = lax.all_to_all(spread, "pairs", split_axis=0, concat_axis=0, tiled=True)
    found = found.reshape(pairs_all, rows * virt)
    earlier = (owner[None, :] == owner[:, None]) & before
    position = owner * capacity + jnp.sum(earlier.astype(jnp.int32), axis=1)
    own_ids = my_group * capacity + jnp.arange(capacity, dtype=jnp.int32)
    own_link = (position[None, :] == own_ids[:, None])
    own_place = jnp.sum(jnp.where(own_link, place[None, :] + 1, 0), axis=1) - 1
    take = (own_place[:, None] == ids[None, :]).astype(jnp.bfloat16)
    return jnp.dot(take, found, preferred_element_type=jnp.float32).reshape(capacity, rows, virt)


def solution(mesh):
    placed = (P(None, "aux", "pairs"), P("aux", None, None), P(), P(), P(), P())
    return jax.shard_map(
        per_device, mesh=mesh, in_specs=placed, out_specs=P("pairs", "aux", None), check_vma=False
    )
```

time: 275 us -> 80.6 us (0.29)
  waiting for transfers between devices: 153 us -> 31.2 us
  blocking collectives: 37.8 us -> 0 us
  matrix products: 24.8 us -> 0.34 us
  local copies, waits for them, and re-layouts: 33.2 us -> 11.1 us
  starting transfers between devices: 7.66 us -> 23 us
  between operations: 14.2 us -> 1.39 us
  Pallas kernels: 0 us -> 8.33 us
    unnamed x3 -> x0, waiting for transfers between devices: 105 us -> none
    all_gather x1 -> x0, waiting for transfers between devices: 41.7 us -> none  [per_device(): lax.all_gather(flipped, 'pairs', axis=0, tiled=True)]
    dynamic_update_slice x8 -> x0, local copies, waits for them, and re-layouts: 27.4 us -> none  [ladder_rows(): running = lax.map(one_slot, whole_tiles)]
    all_to_all x1 -> x3, waiting for transfers between devices: 6.41 us -> 31.2 us  [the longest x1 12.1 us: per_device(): lax.all_to_all(outgoing, ('aux', 'pairs'), split_axis=0, concat_axis=0, t...]
    dot_general x7 -> x2, matrix products: 24.6 us -> 0.34 us  [the longest x1 0.21 us: per_device(): jnp.dot(take, found, preferred_element_type=jnp.float32)]
    all_gather x1 -> x0, blocking collectives: 23.4 us -> none  [ladder_rows(): whole_tiles = lax.all_gather(amp_tiles, 'aux', axis=1, tiled=True)]
    all_to_all x1 -> x3, starting transfers between devices: 7.57 us -> 23 us  [the longest x1 15.6 us: per_device(): lax.all_to_all(outgoing, ('aux', 'pairs'), split_axis=0, concat_axis=0, t...]
    all_to_all x1 -> x0, blocking collectives: 14.4 us -> none  [scale_turn(): lax.all_to_all(scaled, 'aux', split_axis=2, concat_axis=1, tiled=True)]
  transfers between devices with their start and end apart: 3 -> 3, of which waited for: 3 -> 3; matrix products, arithmetic and copies ran while one was open for 0% -> 4% of each run, Pallas kernels for 0% -> 0%
where the time goes in v1:
time: 80.6 us; the launch traced here: 80 us
  waiting for transfers between devices  31.2 us (39%)
  starting transfers between devices  23 us (29%)
  local copies, waits for them, and re-layouts  11.1 us (14%)
  Pallas kernels  8.33 us (10%)
  other arithmetic  4.67 us (6%)
  between operations  1.39 us (2%)
    all_to_all x1, starting transfers between devices, per_device(): lax.all_to_all(outgoing, ('aux', 'pairs'), split_axis=0, concat_axis=0, t...  15.6 us
    all_to_all x1, waiting for transfers between devices, per_device(): lax.all_to_all(outgoing, ('aux', 'pairs'), split_axis=0, concat_axis=0, t...  12.1 us
    all_to_all x1, waiting for transfers between devices, per_device(): lax.all_to_all(partial, 'aux', split_axis=0, concat_axis=0, tiled=True)  10.9 us
    pallas_call x1, Pallas kernels, ladder(): pl.pallas_call(ladder_kernel, grid=(naux // count,), in_specs=[smem, smem...  8.33 us
    all_to_all x1, waiting for transfers between devices, per_device(): lax.all_to_all(spread, 'pairs', split_axis=0, concat_axis=0, tiled=True)  8.21 us
    reshape x2, local copies, waits for them, and re-layouts, per_device(): arrived.reshape(aux, groups, 2, rows, cols).transpose(2, 0, 3, 1, 4)  5.3 us
    all_to_all x1, starting transfers between devices, per_device(): lax.all_to_all(spread, 'pairs', split_axis=0, concat_axis=0, tiled=True)  3.92 us
    all_to_all x1, starting transfers between devices, per_device(): lax.all_to_all(partial, 'aux', split_axis=0, concat_axis=0, tiled=True)  3.43 us
  transfers between devices with their start and end apart: 3, of which 3 were waited for; matrix products, arithmetic and copies ran while one was open for 4% of the time, Pallas kernels for 0%

profile of v1, /device:TPU:1, one launch (start us, length us, event | category | flops | bytes accessed | tf_op | source)
XLA Modules:
  0.0 80.0 jit_solution(15024997278324802083)
XLA Ops:
  0.0 1.3 %iota_minimum_fusion = (s32[32]{0:T(128)S(1)}, s32[]{:T(128)}) fusion(s32[32]{0:T(128)} %param.11), kind=kLoop, calls=%fused_computation.28 | loop fusion | flops 127 | bytes 260 | tf_op jit(solution)/shard_map/min | solution.py:86
  1.3 0.7 iota_compare_fusion.6
  2.6 0.2 convert_reduce_fusion
  2.8 0.7 broadcast_add_fusion.1
  3.5 0.1 convolution_convert_fusion
  3.7 0.9 %broadcast_in_dim.35 = bf16[16,16,2,256]{3,2,1,0:T(2,128)(2,1)} broadcast(bf16[16,2,256]{2,1,0:T(2,128)(2,1)S(1)} %broadcast_in_dim.34), dimensions={1,2,3} | broadcast | bytes 278528 | tf_op jit(solution)/shard_map/broadcast_in_dim | solution.py:97
  4.6 15.6 %all-to-all-start = ((bf16[256,2,256]{2,1,0:T(2,128)(2,1)}), bf16[256,2,256]{2,1,0:T(2,128)(2,1)S(1)}, u32[]{:S(2)}, u32[]{:S(2)}) async-start(bf16[256,2,256]{2,1,0:T(2,128)(2,1)} %bitcast.3), calls=%async_computation | async-start | bytes 524288 | tf_op jit(solution)/shard_map/all_to_all | solution.py:100
  20.9 0.8 %select_reduce_fusion = f32[32]{0:T(128)S(1)} fusion(f32[32]{0:T(128)} %param.9, s32[32]{0:T(128)S(1)} %get-tuple-element.6, pred[32]{0:T(512)(128)(4,1)S(1)} %fusion.11), kind=kLoop, calls=%fused_computation.4 | loop fusion | flops 4064 | bytes 416 | tf_op jit(solution)/shard_map/reduce_sum | solution.py:103
  21.8 1.5 %copy.20.row_e_ref = f32[256,1]{1,0:T(8,128)} copy(f32[256,1]{0,1:T(1,128)} %bitcast.29) | data formatting | bytes 2048 | tf_op jit(solution)/shard_map/broadcast_in_dim | solution.py:71
  23.3 0.6 reduce_sum.81.pair_e_ref
  23.9 12.1 %all-to-all-done = bf16[256,2,256]{2,1,0:T(2,128)(2,1)S(1)} async-done(((bf16[256,2,256]{2,1,0:T(2,128)(2,1)}), bf16[256,2,256]{2,1,0:T(2,128)(2,1)S(1)}, u32[]{:S(2)}, u32[]{:S(2)}) %all-to-all-start) | async-done | bytes 262176 | tf_op jit(solution)/shard_map/all_to_all | solution.py:100
  35.9 1.4 %reshape.89 = bf16[16,16,2,16,16]{4,3,1,0,2:T(8,128)(2,1)S(1)} reshape(bf16[256,2,256]{2,0,1:T(8,128)(2,1)S(1)} %copy.18) | data formatting | bytes 524288 | tf_op jit(solution)/shard_map/reshape | solution.py:101
  37.4 1.9 %copy.19 = bf16[2,16,16,16,16]{4,3,2,1,0:T(8,128)(2,1)} copy(bf16[2,16,16,16,16]{4,2,3,1,0:T(8,128)(2,1)S(1)} %bitcast.27) | data formatting | bytes 524288 | tf_op jit(solution)/shard_map/transpose | solution.py:101
  39.3 3.9 %reshape.90.amp_ref = bf16[2,256,256]{2,1,0:T(8,128)(2,1)} reshape(bf16[2,16,16,16,16]{4,3,2,1,0:T(8,128)(2,1)} %copy.19) | data formatting | bytes 524288 | tf_op jit(solution)/shard_map/reshape | solution.py:101
  43.2 8.3 %ladder.1 = bf16[16,2,16,256]{3,2,1,0:T(8,128)(2,1)} custom-call(s32[1]{0:T(128)} %bitcast.1.same_ref, f32[2]{0:T(128)} %reduce_sum.81.pair_e_ref, bf16[2,256,256]{2,1,0:T(8,128)(2,1)} %reshape.90.amp_ref, bf16[28,256,256]{2,1,0:T(8,128)(2,1)} %b_ref.1, f32[256,1]{1,0:T(8,128)} %copy.20.row_e_ref, f32[1,256]{1,0:T(1,128)} %bitcast.30), custom_call_target="tpu_custom_call" | custom-call | tf_op jit(solution)/shard_map/ladder/pallas_call | solution.py:53
  51.5 3.4 %all-to-all-start.1 = ((bf16[16,2,16,256]{3,2,1,0:T(8,128)(2,1)}), bf16[16,2,16,256]{3,2,1,0:T(8,128)(2,1)S(1)}, u32[]{:S(2)}, u32[]{:S(2)}) async-start(bf16[16,2,16,256]{3,2,1,0:T(8,128)(2,1)} %ladder.1), calls=%async_computation.1 | async-start | bytes 524288 | tf_op jit(solution)/shard_map/all_to_all | solution.py:106
  55.0 0.2 convert_reduce_fusion.2
  55.1 10.9 %all-to-all-done.1 = bf16[16,2,16,256]{3,2,1,0:T(8,128)(2,1)S(1)} async-done(((bf16[16,2,16,256]{3,2,1,0:T(8,128)(2,1)}), bf16[16,2,16,256]{3,2,1,0:T(8,128)(2,1)S(1)}, u32[]{:S(2)}, u32[]{:S(2)}) %all-to-all-start.1) | async-done | bytes 262176 | tf_op jit(solution)/shard_map/all_to_all | solution.py:106
  66.1 0.7 broadcast_in_dim.68
  66.8 3.9 %all-to-all-start.2 = ((bf16[16,2,16,256]{3,2,1,0:T(8,128)(2,1)}), bf16[16,2,16,256]{3,2,1,0:T(8,128)(2,1)S(1)}, u32[]{:S(2)}, u32[]{:S(2)}) async-start(bf16[16,2,16,256]{3,2,1,0:T(8,128)(2,1)} %broadcast_in_dim.68), calls=%async_computation.2 | async-start | bytes 524288 | tf_op jit(solution)/shard_map/all_to_all | solution.py:109
  70.7 0.2 select_reduce_fusion.1
  70.9 8.2 %all-to-all-done.2 = bf16[16,2,16,256]{3,2,1,0:T(8,128)(2,1)S(1)} async-done(((bf16[16,2,16,256]{3,2,1,0:T(8,128)(2,1)}), bf16[16,2,16,256]{3,2,1,0:T(8,128)(2,1)S(1)}, u32[]{:S(2)}, u32[]{:S(2)}) %all-to-all-start.2) | async-done | bytes 262176 | tf_op jit(solution)/shard_map/all_to_all | solution.py:109
  79.1 0.2 fusion
  79.4 0.6 copy.22
  (12 shorter events, 0.2 us)
Async XLA Ops:
  0.0 3.5 %copy-start = (bf16[32,16,16]{0,2,1:T(8,128)(2,1)S(1)}, bf16[32,16,16]{0,2,1:T(8,128)(2,1)}, u32[]{:S(2)}) copy-start(bf16[32,16,16]{0,2,1:T(8,128)(2,1)} %param.6) | copy-start | bytes 49156
  4.6 31.4 %all-to-all-start = ((bf16[256,2,256]{2,1,0:T(2,128)(2,1)}), bf16[256,2,256]{2,1,0:T(2,128)(2,1)S(1)}, u32[]{:S(2)}, u32[]{:S(2)}) async-start(bf16[256,2,256]{2,1,0:T(2,128)(2,1)} %bitcast.3), calls=%async_computation | async-start | bytes 524288 | tf_op jit(solution)/shard_map/all_to_all | solution.py:100
  43.2 11.8 %copy-start.1 = (s32[32]{0:T(128)S(1)}, s32[32]{0:T(128)}, u32[]{:S(2)}) copy-start(s32[32]{0:T(128)} %param.10) | copy-start | bytes 388
  51.5 14.6 %all-to-all-start.1 = ((bf16[16,2,16,256]{3,2,1,0:T(8,128)(2,1)}), bf16[16,2,16,256]{3,2,1,0:T(8,128)(2,1)S(1)}, u32[]{:S(2)}, u32[]{:S(2)}) async-start(bf16[16,2,16,256]{3,2,1,0:T(8,128)(2,1)} %ladder.1), calls=%async_computation.1 | async-start | bytes 524288 | tf_op jit(solution)/shard_map/all_to_all | solution.py:106
  66.8 12.3 %all-to-all-start.2 = ((bf16[16,2,16,256]{3,2,1,0:T(8,128)(2,1)}), bf16[16,2,16,256]{3,2,1,0:T(8,128)(2,1)S(1)}, u32[]{:S(2)}, u32[]{:S(2)}) async-start(bf16[16,2,16,256]{3,2,1,0:T(8,128)(2,1)} %broadcast_in_dim.68), calls=%async_computation.2 | async-start | bytes 524288 | tf_op jit(solution)/shard_map/all_to_all | solution.py:109

commit v2 on v0

v2 whole, which is shorter than its diff:
```python
import jax
import jax.numpy as jnp
from jax import lax
from jax.experimental import pallas as pl
from jax.experimental.pallas import tpu as pltpu
from jax.sharding import Mesh
from jax.sharding import PartitionSpec as P

BF16 = jnp.bfloat16
F32 = jnp.float32
NT = (((1,), (1,)), ((), ()))
VMEM_SPEC = pl.BlockSpec(memory_space=pltpu.VMEM)


def in_vmem(x):
    return pltpu.with_memory_space_constraint(x, pltpu.VMEM)


def iota(shape, dim):
    return lax.broadcasted_iota(jnp.int32, shape, dim)


def swap_matrix(side):
    full = side * side
    turned = (iota((full, full), 0) % side) * side + iota((full, full), 0) // side
    return jnp.where(turned == iota((full, full), 1), 1.0, 0.0).astype(BF16)


def plan_kernel(group_ref, amp_ref, partner_ref, owner_ref, energy_ref, out_ref, take_ref, info_ref, *, side, capacity):
    count = partner_ref.shape[1]
    square = (count, count)
    group = group_ref[...]
    row = iota(square, 0)
    col = iota(square, 1)
    diagonal = row == col
    partner = jnp.broadcast_to(partner_ref[...], square)
    owner = jnp.broadcast_to(owner_ref[...], square)

    def down(x):
        return jnp.sum(jnp.where(diagonal, x, 0), axis=1, keepdims=True)

    leads = (partner > col).astype(jnp.int32)
    fixed = (partner == col).astype(jnp.int32)
    low = jnp.minimum(partner, col)
    lead_rank = jnp.sum(jnp.where(row < low, down(leads), 0), axis=0, keepdims=True)
    fixed_rank = jnp.sum(jnp.where(row < col, down(fixed), 0), axis=0, keepdims=True)
    leaders = jnp.sum(leads[:1], axis=1, keepdims=True)
    late = (col[:1] > partner[:1]).astype(jnp.int32)
    place = jnp.where(fixed[:1] > 0, 2 * leaders + fixed_rank, 2 * lead_rank + late)
    pick = jnp.where(jnp.broadcast_to(place, square) == row, 1.0, 0.0).astype(BF16)
    tiles = lax.dot_general(pick, amp_ref[...], NT, preferred_element_type=F32).astype(BF16)
    out_ref[...] = jnp.dot(tiles, swap_matrix(side), preferred_element_type=F32).astype(BF16)
    slot_rank = jnp.sum(((down(owner) == owner) & (row < col)).astype(jnp.int32), axis=0, keepdims=True)
    position = owner_ref[...] * capacity + slot_rank
    small = (8, count)
    wanted = iota(small, 0) + capacity * jnp.broadcast_to(group[:1, :count], small)
    mine = jnp.where(jnp.broadcast_to(position, small) == wanted, 1.0, 0.0).astype(BF16)
    take_ref[...] = lax.dot_general(mine, pick, NT, preferred_element_type=F32).astype(BF16)
    slots = iota(small, 0) + 2 * jnp.broadcast_to(group[:1, :count], small)
    chosen = jnp.where(jnp.broadcast_to(place, small) == slots, jnp.broadcast_to(energy_ref[...], small), 0.0)
    energies = jnp.broadcast_to(jnp.sum(chosen, axis=1, keepdims=True), (8, 128))
    same = jnp.where(group >= jnp.broadcast_to(leaders, (8, 128)), 1.0, 0.0)
    info_ref[...] = jnp.where(iota((8, 128), 0) == 2, same, energies)


def plan(amplitudes, partner, owner, pair_energy, group, capacity):
    count, side, _ = amplitudes.shape
    amp = jnp.transpose(amplitudes, (1, 2, 0)).reshape(side * side, count)
    return pl.pallas_call(
        lambda *refs: plan_kernel(*refs, side=side, capacity=capacity),
        in_specs=[VMEM_SPEC] * 5,
        out_specs=[VMEM_SPEC] * 3,
        out_shape=[
            jax.ShapeDtypeStruct((count, side * side), BF16),
            jax.ShapeDtypeStruct((8, count), BF16),
            jax.ShapeDtypeStruct((8, 128), F32),
        ],
        compiler_params=pltpu.CompilerParams(vmem_limit_bytes=8 << 20),
        name="plan",
    )(
        jnp.full((8, 128), group, jnp.int32),
        amp,
        partner.reshape(1, count),
        owner.reshape(1, count),
        pair_energy.reshape(1, count),
    )


def ladder_kernel(core_ref, info_ref, virt_ref, own_ref, other_ref, b_ref, out_ref, turned, *, side):
    virt = b_ref.shape[1]
    naux = b_ref.shape[0]
    half_lanes = virt // 2
    per_vector = half_lanes // side
    first_core = jnp.broadcast_to(core_ref[:1, :] == 0, (side, half_lanes))

    def piece(slot, z, core, half):
        rows = pl.ds(z * side, side)
        lanes = pl.ds(half * half_lanes, half_lanes)
        own = own_ref[slot, rows, lanes].astype(F32)
        other = other_ref[slot, rows, lanes].astype(F32)
        return jnp.where(first_core, own, other) if core == 0 else jnp.where(first_core, other, own)

    order = [(slot, half, high) for slot in range(2) for half in range(2) for high in range(2)]
    vectors = []
    for low in range(per_vector):
        z_low, core = low // 2, low % 2
        vectors.append(
            jnp.concatenate(
                [piece(slot, high * (per_vector // 2) + z_low, core, half) for slot, half, high in order], axis=0
            )
        )
    lane_group = iota(vectors[0].shape, 1) // side
    step = 1
    while step < per_vector:
        keep = (lane_group & step) == 0
        shift = step * side
        for i in range(per_vector):
            if i & step:
                continue
            j = i | step
            a, b = vectors[i], vectors[j]
            vectors[i] = jnp.where(keep, a, pltpu.roll(b, shift, 1))
            vectors[j] = jnp.where(keep, pltpu.roll(a, half_lanes - shift, 1), b)
        step *= 2
    for s_low in range(per_vector):
        vector = vectors[s_low].astype(BF16)
        for k, (slot, half, high) in enumerate(order):
            rows = pl.ds((half * per_vector + s_low) * side, side)
            lanes = pl.ds(slot * virt + high * half_lanes, half_lanes)
            turned[rows, lanes] = vector[k * side : (k + 1) * side]
    amp_t = jnp.dot(swap_matrix(side), turned[...], preferred_element_type=F32).astype(BF16)

    half = jnp.dot(
        b_ref[...].reshape(naux * virt, virt), amp_t, preferred_element_type=F32
    ).astype(BF16)
    totals = []
    for slot in range(2):
        total = jnp.zeros((virt, virt), F32)
        for q in range(naux):
            total += lax.dot_general(
                half[q * virt : (q + 1) * virt, slot * virt : (slot + 1) * virt],
                b_ref[q],
                NT,
                preferred_element_type=F32,
            )
        totals.append(total)

    rows_of = jnp.broadcast_to(virt_ref[...], (virt, virt))
    sums = rows_of + rows_of.T
    info = info_ref[...]
    first = totals[0] / (sums - info[0:1, 0:1])
    second = totals[1] / (sums - info[1:2, 0:1])
    same = jnp.broadcast_to(info[2:3, 0:1] > 0.5, (virt, virt))
    blocks = (first.T + jnp.where(same, first, second), second.T + jnp.where(same, second, first))
    share = out_ref.shape[2]
    for slot in range(2):
        out_ref[:, slot] = blocks[slot].astype(BF16).reshape(virt // share, share, virt)


def ladder(core, info, virt_energy, own, other, three_index, aux, side):
    virt = three_index.shape[1]
    return pl.pallas_call(
        lambda *refs: ladder_kernel(*refs, side=side),
        in_specs=[VMEM_SPEC] * 6,
        out_specs=VMEM_SPEC,
        out_shape=jax.ShapeDtypeStruct((aux, 2, virt // aux, virt), BF16),
        scratch_shapes=[pltpu.VMEM((virt, 2 * virt), BF16)],
        compiler_params=pltpu.CompilerParams(vmem_limit_bytes=40 << 20),
        name="ladder",
    )(
        jnp.full((8, 128), core, jnp.int32),
        info,
        virt_energy.reshape(1, virt),
        own,
        other,
        in_vmem(three_index),
    )


def gather_kernel(shares_ref, out_ref):
    total = shares_ref[0].astype(F32)
    for k in range(1, shares_ref.shape[0]):
        total += shares_ref[k].astype(F32)
    done = total.astype(BF16)
    for k in range(out_ref.shape[0]):
        out_ref[k] = done


def gather(shares, groups):
    return pl.pallas_call(
        gather_kernel,
        in_specs=[VMEM_SPEC],
        out_specs=VMEM_SPEC,
        out_shape=jax.ShapeDtypeStruct((groups,) + shares.shape[1:], BF16),
        compiler_params=pltpu.CompilerParams(vmem_limit_bytes=8 << 20),
        name="gather",
    )(shares)


def per_device(amplitudes, three_index, virt_energy, pair_energy, owner, partner):
    aux_axes = ("z", "core")
    aux = lax.axis_size(aux_axes)
    depth = lax.axis_size("z")
    groups = lax.axis_size("pairs")
    pairs_all, side, _ = amplitudes.shape
    virt = three_index.shape[1]
    capacity = 2 * (pairs_all // groups)
    tiles, take, info = plan(amplitudes, partner, owner, pair_energy, lax.axis_index("pairs"), capacity)
    outgoing = jnp.broadcast_to(
        tiles.reshape(1, groups, 2, side * side), (depth, groups, 2, side * side)
    ).reshape(depth * groups, 2, side * side)
    arrived = lax.all_to_all(outgoing, ("z", "pairs"), split_axis=0, concat_axis=0, tiled=True)
    own = jnp.transpose(arrived, (1, 0, 2))
    other = lax.ppermute(own, "core", [(0, 1), (1, 0)])
    partial = ladder(lax.axis_index("core"), info, virt_energy, own, other, three_index, aux, side)
    shares = lax.all_to_all(partial, aux_axes, split_axis=0, concat_axis=0, tiled=True)
    spread = gather(shares, groups)
    found = lax.all_to_all(spread, "pairs", split_axis=0, concat_axis=0, tiled=True)
    found = found.reshape(pairs_all, side * virt)
    return jnp.dot(take[:capacity], found, preferred_element_type=F32).reshape(capacity, side, virt)


def solution(mesh):
    groups = mesh.shape["pairs"]
    devices = mesh.devices.reshape(mesh.shape["aux"] // 2, 2, groups)
    split = Mesh(devices, ("z", "core", "pairs"))
    aux = ("z", "core")
    placed = (P(None, aux, "pairs"), P(aux, None, None), P(), P(), P(), P())
    return jax.shard_map(
        per_device, mesh=split, in_specs=placed, out_specs=P("pairs", aux, None), check_vma=False
    )
```

time: 275 us -> 68.3 us (0.25)
  waiting for transfers between devices: 153 us -> 0.99 us
  local copies, waits for them, and re-layouts: 33.2 us -> 6.27 us
  matrix products: 24.8 us -> 0.19 us
  blocking collectives: 37.8 us -> 53.3 us
  between operations: 14.2 us -> 0.04 us
  starting transfers between devices: 7.66 us -> 2.19 us
  Pallas kernels: 0 us -> 4.96 us
  other arithmetic: 3.58 us -> 0 us
    unnamed x3 -> x0, waiting for transfers between devices: 105 us -> none
    all_gather x1 -> x0, waiting for transfers between devices: 41.7 us -> none  [per_device(): lax.all_gather(flipped, 'pairs', axis=0, tiled=True)]
    all_to_all x1 -> x3, blocking collectives: 14.4 us -> 53.3 us  [the longest x1 27.4 us: per_device(): lax.all_to_all(outgoing, ('z', 'pairs'), split_axis=0, concat_axis=0, til...]
    dynamic_update_slice x8 -> x0, local copies, waits for them, and re-layouts: 27.4 us -> none  [ladder_rows(): running = lax.map(one_slot, whole_tiles)]
    dot_general x7 -> x1, matrix products: 24.6 us -> 0.19 us  [per_device(): jnp.dot(take[:capacity], found, preferred_element_type=F32)]
    all_gather x1 -> x0, blocking collectives: 23.4 us -> none  [ladder_rows(): whole_tiles = lax.all_gather(amp_tiles, 'aux', axis=1, tiled=True)]
    all_to_all x1 -> x0, starting transfers between devices: 7.57 us -> none  [per_device(): lax.all_to_all(outgoing, 'pairs', split_axis=0, concat_axis=3, tiled=True)]
    all_to_all x1 -> x0, waiting for transfers between devices: 6.41 us -> none  [per_device(): lax.all_to_all(outgoing, 'pairs', split_axis=0, concat_axis=3, tiled=True)]
  transfers between devices with their start and end apart: 3 -> 1, of which waited for: 3 -> 1; matrix products, arithmetic and copies ran while one was open for 0% -> 0% of each run, Pallas kernels for 0% -> 0%
where the time goes in v2:
time: 68.3 us; the launch traced here: 68 us
  blocking collectives  53.3 us (78%)
  local copies, waits for them, and re-layouts  6.27 us (9%)
  Pallas kernels  4.96 us (7%)
  starting transfers between devices  2.19 us (3%)
  waiting for transfers between devices  0.99 us (1%)
    all_to_all x1, blocking collectives, per_device(): lax.all_to_all(outgoing, ('z', 'pairs'), split_axis=0, concat_axis=0, til...  27.4 us
    all_to_all x1, blocking collectives, per_device(): lax.all_to_all(partial, aux_axes, split_axis=0, concat_axis=0, tiled=True)  14.5 us
    all_to_all x1, blocking collectives, per_device(): lax.all_to_all(spread, 'pairs', split_axis=0, concat_axis=0, tiled=True)  11.4 us
    unnamed x12, local copies, waits for them, and re-layouts  5.52 us
    pallas_call x1, Pallas kernels, ladder(): pl.pallas_call(lambda *refs: ladder_kernel(*refs, side=side), in_specs=[V...  4.58 us
    ppermute x1, starting transfers between devices, per_device(): other = lax.ppermute(own, 'core', [(0, 1), (1, 0)])  2.19 us
  transfers between devices with their start and end apart: 1, of which 1 were waited for; matrix products, arithmetic and copies ran while one was open for 0% of the time, Pallas kernels for 0%

profile of v2, /device:TPU:1, one launch (start us, length us, event | category | flops | bytes accessed | tf_op | source)
XLA Modules:
  0.0 68.0 jit_solution(3089480291509473480)
XLA Ops:
  0.0 0.0 copy-start.1
  0.0 0.8 %copy-done.1 = bf16[32,16,16]{0,2,1:T(8,128)(2,1)S(1)} copy-done((bf16[32,16,16]{0,2,1:T(8,128)(2,1)S(1)}, bf16[32,16,16]{0,2,1:T(8,128)(2,1)}, u32[]{:S(2)}) %copy-start.1) | copy-done | bytes 16408
  0.8 0.0 copy-start.3
  0.8 0.7 copy-done.3
  1.5 0.0 copy-start.4
  1.5 0.7 copy-done.4
  2.2 0.0 copy-start.5
  2.2 0.7 copy-done.5
  2.8 0.3 plan.1
  3.2 0.1 broadcast_in_dim.16
  3.3 27.4 %all_to_all.15 = bf16[128,2,256]{2,1,0:T(2,128)(2,1)S(1)} all-to-all(bf16[128,2,256]{2,1,0:T(2,128)(2,1)S(1)} %bitcast.33), channel_id=1, replica_groups=mesh['z'=8,'core'=2,'pairs'=16] {'z','pairs'}, dimensions={0} | all-to-all | bytes 262144 | tf_op jit(solution)/shard_map/all_to_all | solution.py:212
  30.6 2.2 %collective-permute-start = (bf16[2,128,256]{2,1,0:T(8,128)(2,1)S(1)}, bf16[2,128,256]{2,1,0:T(8,128)(2,1)S(1)}, u32[]{:S(2)}, u32[]{:S(2)}) collective-permute-start(bf16[2,128,256]{2,1,0:T(8,128)(2,1)S(1)} %bitcast.26), channel_id=1, source_target_pairs={{0,16},{16,0},{1,17},{17,1},{2,18},{18,2},{3,19},{19,3},{4,20},{20... | collective-permute-start | bytes 393224 | tf_op jit(solution)/shard_map/ppermute | solution.py:214
  32.8 1.0 %collective-permute-done.refs_4_ = bf16[2,128,256]{2,1,0:T(8,128)(2,1)S(1)} collective-permute-done((bf16[2,128,256]{2,1,0:T(8,128)(2,1)S(1)}, bf16[2,128,256]{2,1,0:T(8,128)(2,1)S(1)}, u32[]{:S(2)}, u32[]{:S(2)}) %collective-permute-start) | collective-permute-done | bytes 131104 | tf_op jit(solution)/shard_map/ppermute | solution.py:214
  33.8 0.0 copy-start
  33.8 2.0 %copy-done = bf16[28,256,256]{2,1,0:T(8,128)(2,1)S(1)} copy-done((bf16[28,256,256]{2,1,0:T(8,128)(2,1)S(1)}, bf16[28,256,256]{2,1,0:T(8,128)(2,1)}, u32[]{:S(2)}) %copy-start) | copy-done | bytes 3670040
  35.9 0.0 copy-start.2
  35.9 0.7 copy-done.2
  36.5 4.6 %ladder.1 = bf16[16,2,16,256]{3,2,1,0:T(8,128)(2,1)S(1)} custom-call(s32[8,128]{1,0:T(8,128)S(1)} %broadcast_in_dim.14.refs_0_, f32[8,128]{1,0:T(8,128)S(1)} %get-tuple-element.9.refs_1_, f32[1,256]{1,0:T(1,128)S(1)} %bitcast.29, bf16[2,128,256]{2,1,0:T(8,128)(2,1)S(1)} %bitcast.27, bf16[2,128,256]{2,1,0:T(8,128)(2,1)S(1)} %collective-permute-done.refs_4_, ...), custom_call_target="tpu_custom_call" | custom-call | tf_op jit(solution)/shard_map/ladder/pallas_call | solution.py:162
  41.1 14.5 %all_to_all.16.shares_ref = bf16[16,2,16,256]{3,2,1,0:T(8,128)(2,1)S(1)} all-to-all(bf16[16,2,16,256]{3,2,1,0:T(8,128)(2,1)S(1)} %ladder.1), channel_id=1, replica_groups=mesh['z'=8,'core'=2,'pairs'=16] {'z','core'}, dimensions={0} | all-to-all | bytes 524288 | tf_op jit(solution)/shard_map/all_to_all | solution.py:216
  55.7 11.4 %all_to_all.17 = bf16[16,2,16,256]{3,2,1,0:T(8,128)(2,1)S(1)} all-to-all(bf16[16,2,16,256]{3,2,1,0:T(8,128)(2,1)S(1)} %gather.1), channel_id=1, replica_groups=mesh['z'=8,'core'=2,'pairs'=16] {'pairs'}, dimensions={0} | all-to-all | bytes 524288 | tf_op jit(solution)/shard_map/all_to_all | solution.py:218
  67.1 0.2 fusion
  67.3 0.6 copy.14
  (5 shorter events, 0.1 us)
Async XLA Ops:
  0.0 0.8 %copy-start.1 = (bf16[32,16,16]{0,2,1:T(8,128)(2,1)S(1)}, bf16[32,16,16]{0,2,1:T(8,128)(2,1)}, u32[]{:S(2)}) copy-start(bf16[32,16,16]{0,2,1:T(8,128)(2,1)} %param.6) | copy-start | bytes 49156
  0.8 0.7 copy-start.3
  1.5 0.7 copy-start.4
  2.2 0.7 copy-start.5
  30.6 3.2 %collective-permute-start = (bf16[2,128,256]{2,1,0:T(8,128)(2,1)S(1)}, bf16[2,128,256]{2,1,0:T(8,128)(2,1)S(1)}, u32[]{:S(2)}, u32[]{:S(2)}) collective-permute-start(bf16[2,128,256]{2,1,0:T(8,128)(2,1)S(1)} %bitcast.26), channel_id=1, source_target_pairs={{0,16},{16,0},{1,17},{17,1},{2,18},{18,2},{3,19},{19,3},{4,20},{20... | collective-permute-start | bytes 393224 | tf_op jit(solution)/shard_map/ppermute | solution.py:214
  33.8 2.0 %copy-start = (bf16[28,256,256]{2,1,0:T(8,128)(2,1)S(1)}, bf16[28,256,256]{2,1,0:T(8,128)(2,1)}, u32[]{:S(2)}) copy-start(bf16[28,256,256]{2,1,0:T(8,128)(2,1)} %refs_5_.1) | copy-start | bytes 11010052
  35.9 0.7 copy-start.2

commit v3 on v2

v3 whole, which is shorter than its diff:
```python
import jax
import jax.numpy as jnp
from jax import lax
from jax.experimental import pallas as pl
from jax.experimental.pallas import tpu as pltpu
from jax.sharding import Mesh
from jax.sharding import PartitionSpec as P

BF16 = jnp.bfloat16
F32 = jnp.float32
NT = (((1,), (1,)), ((), ()))
HEAD = 8
HEAD_PARTS = 2
REST_PARTS = 4
VMEM_SPEC = pl.BlockSpec(memory_space=pltpu.VMEM)
HBM_SPEC = pl.BlockSpec(memory_space=pltpu.HBM)


def in_hbm(x):
    return pltpu.with_memory_space_constraint(x, pltpu.HBM)


def iota(shape, dim):
    return lax.broadcasted_iota(jnp.int32, shape, dim)


def swap_matrix(side):
    full = side * side
    turned = (iota((full, full), 0) % side) * side + iota((full, full), 0) // side
    return jnp.where(turned == iota((full, full), 1), 1.0, 0.0).astype(BF16)


def plan_kernel(
    group_ref,
    amp_hbm,
    partner_hbm,
    owner_hbm,
    energy_hbm,
    virt_hbm,
    three_hbm,
    out_ref,
    info_ref,
    virt_ref,
    head_ref,
    amp_ref,
    partner_ref,
    owner_ref,
    energy_ref,
    sems,
    *,
    side,
    capacity,
):
    sources = (partner_hbm, owner_hbm, amp_hbm, energy_hbm, virt_hbm)
    targets = (partner_ref, owner_ref, amp_ref, energy_ref, virt_ref)
    copies = [pltpu.make_async_copy(a, b, sems.at[i]) for i, (a, b) in enumerate(zip(sources, targets))]
    part = head_ref.shape[0] // HEAD_PARTS
    for i in range(HEAD_PARTS):
        rows = pl.ds(i * part, part)
        copies.append(pltpu.make_async_copy(three_hbm.at[rows], head_ref.at[rows], sems.at[len(sources) + i]))
    for copy in copies:
        copy.start()
    count = partner_ref.shape[1]
    square = (count, count)
    group = group_ref[...]
    row = iota(square, 0)
    col = iota(square, 1)
    diagonal = row == col
    swap = swap_matrix(side)
    copies[0].wait()
    copies[1].wait()
    partner = jnp.broadcast_to(partner_ref[...], square)
    owner = jnp.broadcast_to(owner_ref[...], square)

    def down(x):
        return jnp.sum(jnp.where(diagonal, x, 0), axis=1, keepdims=True)

    leads = (partner > col).astype(jnp.int32)
    fixed = (partner == col).astype(jnp.int32)
    low = jnp.minimum(partner, col)
    lead_rank = jnp.sum(jnp.where(row < low, down(leads), 0), axis=0, keepdims=True)
    fixed_rank = jnp.sum(jnp.where(row < col, down(fixed), 0), axis=0, keepdims=True)
    leaders = jnp.sum(leads[:1], axis=1, keepdims=True)
    late = (col[:1] > partner[:1]).astype(jnp.int32)
    place = jnp.where(fixed[:1] > 0, 2 * leaders + fixed_rank, 2 * lead_rank + late)
    pick = jnp.where(jnp.broadcast_to(place, square) == row, 1.0, 0.0).astype(BF16)
    copies[2].wait()
    tiles = lax.dot_general(pick, amp_ref[...], NT, preferred_element_type=F32).astype(BF16)
    out_ref[...] = jnp.dot(tiles, swap, preferred_element_type=F32).astype(BF16)
    slot_rank = jnp.sum(((down(owner) == owner) & (row < col)).astype(jnp.int32), axis=0, keepdims=True)
    position = owner_ref[...] * capacity + slot_rank
    small = (8, count)
    wide = (8, 128)
    my_group = jnp.broadcast_to(group[:1, :count], small)
    mine = jnp.broadcast_to(position, small) == iota(small, 0) + capacity * my_group
    found = jnp.sum(jnp.where(mine, jnp.broadcast_to(place + 1, small), 0), axis=1, keepdims=True)
    copies[3].wait()
    copies[4].wait()
    slots = iota(small, 0) + 2 * my_group
    chosen = jnp.where(jnp.broadcast_to(place, small) == slots, jnp.broadcast_to(energy_ref[...], small), 0.0)
    energies = jnp.broadcast_to(jnp.sum(chosen, axis=1, keepdims=True), wide)
    same = jnp.where(group >= jnp.broadcast_to(leaders, wide), 1.0, 0.0)
    info_ref[0] = jnp.where(iota(wide, 0) == 2, same, energies)
    info_ref[1] = jnp.broadcast_to(found, wide).astype(F32)
    for copy in copies[len(sources) :]:
        copy.wait()


def plan(amplitudes, partner, owner, pair_energy, virt_energy, three_index, group, capacity):
    count, side, _ = amplitudes.shape
    virt = virt_energy.shape[0]
    amp = jnp.transpose(amplitudes, (1, 2, 0)).reshape(side * side, count)
    return pl.pallas_call(
        lambda *refs: plan_kernel(*refs, side=side, capacity=capacity),
        in_specs=[VMEM_SPEC] + [HBM_SPEC] * 6,
        out_specs=[VMEM_SPEC] * 4,
        out_shape=[
            jax.ShapeDtypeStruct((count, side * side), BF16),
            jax.ShapeDtypeStruct((2, 8, 128), F32),
            jax.ShapeDtypeStruct((1, virt), F32),
            jax.ShapeDtypeStruct((HEAD,) + three_index.shape[1:], BF16),
        ],
        scratch_shapes=[
            pltpu.VMEM((side * side, count), BF16),
            pltpu.VMEM((1, count), jnp.int32),
            pltpu.VMEM((1, count), jnp.int32),
            pltpu.VMEM((1, count), F32),
            pltpu.SemaphoreType.DMA((5 + HEAD_PARTS,)),
        ],
        compiler_params=pltpu.CompilerParams(vmem_limit_bytes=8 << 20),
        name="plan",
    )(
        jnp.full((8, 128), group, jnp.int32),
        in_hbm(amp),
        in_hbm(partner.reshape(1, count)),
        in_hbm(owner.reshape(1, count)),
        in_hbm(pair_energy.reshape(1, count)),
        in_hbm(virt_energy.reshape(1, virt)),
        in_hbm(three_index),
    )


def ladder_kernel(core_ref, info_ref, virt_ref, own_ref, other_ref, head_ref, three_hbm, keep_ref, send_ref, turned, rest_ref, sems, *, side):
    virt = head_ref.shape[1]
    head = head_ref.shape[0]
    part = rest_ref.shape[0] // REST_PARTS
    copies = []
    for i in range(REST_PARTS):
        source = three_hbm.at[pl.ds(head + i * part, part)]
        copies.append(pltpu.make_async_copy(source, rest_ref.at[pl.ds(i * part, part)], sems.at[i]))
        copies[-1].start()
    half_lanes = virt // 2
    per_vector = half_lanes // side
    first_core = jnp.broadcast_to(core_ref[:1, :] == 0, (side, half_lanes))

    def piece(slot, z, core, half):
        rows = pl.ds(z * side, side)
        lanes = pl.ds(half * half_lanes, half_lanes)
        own = own_ref[slot, rows, lanes].astype(F32)
        other = other_ref[slot, rows, lanes].astype(F32)
        return jnp.where(first_core, own, other) if core == 0 else jnp.where(first_core, other, own)

    order = [(slot, half, high) for slot in range(2) for half in range(2) for high in range(2)]
    vectors = []
    for low in range(per_vector):
        z_low, core = low // 2, low % 2
        vectors.append(
            jnp.concatenate(
                [piece(slot, high * (per_vector // 2) + z_low, core, half) for slot, half, high in order], axis=0
            )
        )
    lane_group = iota(vectors[0].shape, 1) // side
    step = 1
    while step < per_vector:
        keep = (lane_group & step) == 0
        shift = step * side
        for i in range(per_vector):
            if i & step:
                continue
            j = i | step
            a, b = vectors[i], vectors[j]
            vectors[i] = jnp.where(keep, a, pltpu.roll(b, shift, 1))
            vectors[j] = jnp.where(keep, pltpu.roll(a, half_lanes - shift, 1), b)
        step *= 2
    for s_low in range(per_vector):
        vector = vectors[s_low].astype(BF16)
        for k, (slot, half, high) in enumerate(order):
            rows = pl.ds((half * per_vector + s_low) * side, side)
            lanes = pl.ds(slot * virt + high * half_lanes, half_lanes)
            turned[rows, lanes] = vector[k * side : (k + 1) * side]
    amp_t = jnp.dot(swap_matrix(side), turned[...], preferred_element_type=F32).astype(BF16)

    totals = [jnp.zeros((virt, virt), F32)] * 2
    for i in range(REST_PARTS + 1):
        if i == 0:
            block_ref = head_ref
        else:
            copies[i - 1].wait()
            block_ref = rest_ref.at[pl.ds((i - 1) * part, part)]
        count = block_ref.shape[0]
        rows = block_ref[...].reshape(count * virt, virt)
        half = jnp.dot(rows, amp_t, preferred_element_type=F32).astype(BF16)
        for slot in range(2):
            for q in range(count):
                totals[slot] = totals[slot] + lax.dot_general(
                    half[q * virt : (q + 1) * virt, slot * virt : (slot + 1) * virt],
                    block_ref[q],
                    NT,
                    preferred_element_type=F32,
                )

    rows_of = jnp.broadcast_to(virt_ref[...], (virt, virt))
    sums = rows_of + rows_of.T
    info = info_ref[0]
    first = totals[0] / (sums - info[0:1, 0:1])
    second = totals[1] / (sums - info[1:2, 0:1])
    same = jnp.broadcast_to(info[2:3, 0:1] > 0.5, (virt, virt))
    blocks = (first.T + jnp.where(same, first, second), second.T + jnp.where(same, second, first))
    on_first = jnp.broadcast_to(core_ref[:1, :1] == 0, (virt, virt))
    keep_ref[...] = jnp.where(on_first, blocks[0], blocks[1])
    send_ref[...] = jnp.where(on_first, blocks[1], blocks[0])


def ladder(core, info, virt_row, own, other, head, three_index, side):
    naux, virt, _ = three_index.shape
    return pl.pallas_call(
        lambda *refs: ladder_kernel(*refs, side=side),
        in_specs=[VMEM_SPEC] * 6 + [HBM_SPEC],
        out_specs=[VMEM_SPEC] * 2,
        out_shape=[jax.ShapeDtypeStruct((virt, virt), F32)] * 2,
        scratch_shapes=[
            pltpu.VMEM((virt, 2 * virt), BF16),
            pltpu.VMEM((naux - HEAD, virt, virt), BF16),
            pltpu.SemaphoreType.DMA((REST_PARTS,)),
        ],
        compiler_params=pltpu.CompilerParams(vmem_limit_bytes=40 << 20),
        name="ladder",
    )(
        jnp.full((8, 128), core, jnp.int32),
        info,
        virt_row,
        own,
        other,
        head,
        in_hbm(three_index),
    )


def merge_kernel(kept_ref, came_ref, out_ref):
    out_ref[...] = (kept_ref[...] + came_ref[...]).astype(BF16).reshape(out_ref.shape)


def merge(kept, came, aux):
    virt = kept.shape[0]
    return pl.pallas_call(
        merge_kernel,
        in_specs=[VMEM_SPEC] * 2,
        out_specs=VMEM_SPEC,
        out_shape=jax.ShapeDtypeStruct((aux, virt // aux, virt), BF16),
        compiler_params=pltpu.CompilerParams(vmem_limit_bytes=8 << 20),
        name="merge",
    )(kept, came)


def gather_kernel(shares_ref, out_ref):
    for core in range(2):
        total = shares_ref[core].astype(F32)
        for k in range(core + 2, shares_ref.shape[0], 2):
            total += shares_ref[k].astype(F32)
        done = total.astype(BF16)
        for k in range(out_ref.shape[0]):
            out_ref[k, core] = done


def gather(shares, groups):
    return pl.pallas_call(
        gather_kernel,
        in_specs=[VMEM_SPEC],
        out_specs=VMEM_SPEC,
        out_shape=jax.ShapeDtypeStruct((groups, 2) + shares.shape[1:], BF16),
        compiler_params=pltpu.CompilerParams(vmem_limit_bytes=8 << 20),
        name="gather",
    )(shares)


def select_kernel(info_ref, found_ref, out_ref):
    for k in range(out_ref.shape[0]):
        index = info_ref[1, k, 0].astype(jnp.int32)
        block = found_ref[jnp.maximum(index - 1, 0)].astype(F32)
        out_ref[k] = jnp.where(index > 0, block, 0.0)


def select(info, found, capacity):
    return pl.pallas_call(
        select_kernel,
        in_specs=[VMEM_SPEC] * 2,
        out_specs=VMEM_SPEC,
        out_shape=jax.ShapeDtypeStruct((capacity,) + found.shape[1:], F32),
        compiler_params=pltpu.CompilerParams(vmem_limit_bytes=8 << 20),
        name="select",
    )(info, found)


def per_device(amplitudes, three_index, virt_energy, pair_energy, owner, partner):
    aux_axes = ("z", "core")
    swap = [(0, 1), (1, 0)]
    aux = lax.axis_size(aux_axes)
    depth = lax.axis_size("z")
    groups = lax.axis_size("pairs")
    core = lax.axis_index("core")
    pairs_all, side, _ = amplitudes.shape
    virt = three_index.shape[1]
    capacity = 2 * (pairs_all // groups)
    tiles, info, virt_row, head = plan(
        amplitudes, partner, owner, pair_energy, virt_energy, three_index, lax.axis_index("pairs"), capacity
    )
    outgoing = jnp.broadcast_to(
        tiles.reshape(1, groups, 2, side * side), (depth, groups, 2, side * side)
    ).reshape(depth * groups, 2, side * side)
    arrived = lax.all_to_all(outgoing, ("z", "pairs"), split_axis=0, concat_axis=0, tiled=True)
    own = jnp.transpose(arrived, (1, 0, 2))
    other = lax.ppermute(own, "core", swap)
    keep, send = ladder(core, info, virt_row, own, other, head, three_index, side)
    partial = merge(keep, lax.ppermute(send, "core", swap), aux)
    shares = lax.all_to_all(partial, aux_axes, split_axis=0, concat_axis=0, tiled=True)
    spread = gather(shares, groups)
    found = lax.all_to_all(spread, "pairs", split_axis=0, concat_axis=0, tiled=True)
    return select(info, found.reshape(pairs_all, side, virt), capacity)


def solution(mesh):
    groups = mesh.shape["pairs"]
    devices = mesh.devices.reshape(mesh.shape["aux"] // 2, 2, groups)
    split = Mesh(devices, ("z", "core", "pairs"))
    aux = ("z", "core")
    placed = (P(None, aux, "pairs"), P(aux, None, None), P(), P(), P(), P())
    return jax.shard_map(
        per_device, mesh=split, in_specs=placed, out_specs=P("pairs", aux, None), check_vma=False
    )
```

time: 68.3 us -> 62.5 us (0.915)
  local copies, waits for them, and re-layouts: 6.27 us -> 0.1 us
  blocking collectives: 53.3 us -> 50.4 us
  Pallas kernels: 4.96 us -> 6.91 us
  waiting for transfers between devices: 0.99 us -> 2.16 us
    unnamed x12 -> x0, local copies, waits for them, and re-layouts: 5.52 us -> none
    all_to_all x1, blocking collectives: 14.5 us -> 12 us  [per_device(): lax.all_to_all(partial, aux_axes, split_axis=0, concat_axis=0, tiled=True)]
    ppermute x1 -> x2, waiting for transfers between devices: 0.99 us -> 2.16 us  [the longest x1 1.17 us: per_device(): partial = merge(keep, lax.ppermute(send, 'core', swap), aux)]
    pallas_call x1, Pallas kernels: 0.34 us -> 1.37 us  [plan(): pl.pallas_call(lambda *refs: plan_kernel(*refs, side=side, capacity=capac...]
    pallas_call x0 -> x2, Pallas kernels: none -> 0.71 us  [the longest x1 0.68 us: select(): pl.pallas_call(select_kernel, in_specs=[VMEM_SPEC] * 2, out_specs=VMEM_SP...]
    ppermute x1 -> x2, starting transfers between devices: 2.19 us -> 2.64 us  [the longest x1 2.19 us: per_device(): other = lax.ppermute(own, 'core', swap)]
  transfers between devices with their start and end apart: 1 -> 2, of which waited for: 1 -> 2; matrix products, arithmetic and copies ran while one was open for 0% -> 0% of each run, Pallas kernels for 0% -> 0%
where the time goes in v3:
time: 62.5 us; the launch traced here: 62.3 us
  blocking collectives  50.4 us (81%)
  Pallas kernels  6.91 us (11%)
  starting transfers between devices  2.64 us (4%)
  waiting for transfers between devices  2.16 us (3%)
    all_to_all x1, blocking collectives, per_device(): lax.all_to_all(outgoing, ('z', 'pairs'), split_axis=0, concat_axis=0, til...  27.4 us
    all_to_all x1, blocking collectives, per_device(): lax.all_to_all(partial, aux_axes, split_axis=0, concat_axis=0, tiled=True)  12 us
    all_to_all x1, blocking collectives, per_device(): lax.all_to_all(spread, 'pairs', split_axis=0, concat_axis=0, tiled=True)  11.1 us
    pallas_call x1, Pallas kernels, ladder(): pl.pallas_call(lambda *refs: ladder_kernel(*refs, side=side), in_specs=[V...  4.81 us
    ppermute x1, starting transfers between devices, per_device(): other = lax.ppermute(own, 'core', swap)  2.19 us
    pallas_call x1, Pallas kernels, plan(): pl.pallas_call(lambda *refs: plan_kernel(*refs, side=side, capacity=capac...  1.37 us
  transfers between devices with their start and end apart: 2, of which 2 were waited for; matrix products, arithmetic and copies ran while one was open for 0% of the time, Pallas kernels for 0%

profile of v3, /device:TPU:1, one launch (start us, length us, event | category | flops | bytes accessed | tf_op | source)
XLA Modules:
  0.0 62.3 jit_solution(9018437320793248494)
XLA Ops:
  0.0 1.4 %plan.1 = (bf16[32,256]{1,0:T(8,128)(2,1)S(1)}, f32[2,8,128]{2,1,0:T(8,128)S(1)}, f32[1,256]{1,0:T(1,128)S(1)}, bf16[8,256,256]{2,1,0:T(8,128)(2,1)S(1)}) custom-call(s32[8,128]{1,0:T(8,128)S(1)} %broadcast_in_dim.13.refs_0_, bf16[256,32]{1,0:T(8,128)(2,1)} %bitcast.16, s32[1,32]{1,0:T(1,128)} %bitcast.18, s32[1,32]{1,0:T(1,128)} %bitcast.19, ...), custom_call_target="tpu_custom_call" | custom-call | tf_op jit(solution)/shard_map/plan/pallas_call | solution.py:113
  1.4 0.1 broadcast_in_dim.16
  1.5 27.4 %all_to_all.15 = bf16[128,2,256]{2,1,0:T(2,128)(2,1)S(1)} all-to-all(bf16[128,2,256]{2,1,0:T(2,128)(2,1)S(1)} %bitcast.15), channel_id=1, replica_groups=mesh['z'=8,'core'=2,'pairs'=16] {'z','pairs'}, dimensions={0} | all-to-all | bytes 262144 | tf_op jit(solution)/shard_map/all_to_all | solution.py:320
  28.9 2.2 %collective-permute-start = (bf16[2,128,256]{2,1,0:T(8,128)(2,1)S(1)}, bf16[2,128,256]{2,1,0:T(8,128)(2,1)S(1)}, u32[]{:S(2)}, u32[]{:S(2)}) collective-permute-start(bf16[2,128,256]{2,1,0:T(8,128)(2,1)S(1)} %bitcast.13), channel_id=1, source_target_pairs={{0,16},{16,0},{1,17},{17,1},{2,18},{18,2},{3,19},{19,3},{4,20},{20... | collective-permute-start | bytes 393224 | tf_op jit(solution)/shard_map/ppermute | solution.py:322
  31.1 1.0 %collective-permute-done.refs_4_ = bf16[2,128,256]{2,1,0:T(8,128)(2,1)S(1)} collective-permute-done((bf16[2,128,256]{2,1,0:T(8,128)(2,1)S(1)}, bf16[2,128,256]{2,1,0:T(8,128)(2,1)S(1)}, u32[]{:S(2)}, u32[]{:S(2)}) %collective-permute-start) | collective-permute-done | bytes 131104 | tf_op jit(solution)/shard_map/ppermute | solution.py:322
  32.0 4.8 %ladder.1 = (f32[256,256]{1,0:T(8,128)S(1)}, f32[256,256]{1,0:T(8,128)S(1)}) custom-call(s32[8,128]{1,0:T(8,128)S(1)} %broadcast_in_dim.14.refs_0_, f32[2,8,128]{2,1,0:T(8,128)S(1)} %get-tuple-element.11.refs_1_.info_ref, f32[1,256]{1,0:T(1,128)S(1)} %get-tuple-element.12.refs_2_, bf16[2,128,256]{2,1,0:T(8,128)(2,1)S(1)} %bitcast.14, ...), custom_call_target="tpu_custom_call" | custom-call | tf_op jit(solution)/shard_map/ladder/pallas_call | solution.py:226
  36.9 0.4 collective-permute-start.1
  37.3 1.2 %collective-permute-done.1.came_ref = f32[256,256]{1,0:T(8,128)S(1)} collective-permute-done((f32[256,256]{1,0:T(8,128)S(1)}, f32[256,256]{1,0:T(8,128)S(1)}, u32[]{:S(2)}, u32[]{:S(2)}) %collective-permute-start.1) | collective-permute-done | bytes 262176 | tf_op jit(solution)/shard_map/ppermute | solution.py:324
  38.5 12.0 %all_to_all.16.shares_ref = bf16[16,16,256]{2,1,0:T(8,128)(2,1)S(1)} all-to-all(bf16[16,16,256]{2,1,0:T(8,128)(2,1)S(1)} %merge.1), channel_id=1, replica_groups=mesh['z'=8,'core'=2,'pairs'=16] {'z','core'}, dimensions={0} | all-to-all | bytes 262144 | tf_op jit(solution)/shard_map/all_to_all | solution.py:325
  50.5 11.1 %all_to_all.17 = bf16[16,2,16,256]{3,2,1,0:T(8,128)(2,1)S(1)} all-to-all(bf16[16,2,16,256]{3,2,1,0:T(8,128)(2,1)S(1)} %gather.1), channel_id=1, replica_groups=mesh['z'=8,'core'=2,'pairs'=16] {'pairs'}, dimensions={0} | all-to-all | bytes 524288 | tf_op jit(solution)/shard_map/all_to_all | solution.py:327
  61.6 0.7 %select.1 = f32[4,16,256]{2,1,0:T(8,128)} custom-call(f32[2,8,128]{2,1,0:T(8,128)S(1)} %get-tuple-element.11.refs_1_.info_ref, bf16[32,16,256]{2,1,0:T(8,128)(2,1)S(1)} %bitcast.12), custom_call_target="tpu_custom_call" | custom-call | tf_op jit(solution)/shard_map/select/pallas_call | solution.py:294
  (6 shorter events, 0.1 us)
Async XLA Ops:
  28.9 3.2 %collective-permute-start = (bf16[2,128,256]{2,1,0:T(8,128)(2,1)S(1)}, bf16[2,128,256]{2,1,0:T(8,128)(2,1)S(1)}, u32[]{:S(2)}, u32[]{:S(2)}) collective-permute-start(bf16[2,128,256]{2,1,0:T(8,128)(2,1)S(1)} %bitcast.13), channel_id=1, source_target_pairs={{0,16},{16,0},{1,17},{17,1},{2,18},{18,2},{3,19},{19,3},{4,20},{20... | collective-permute-start | bytes 393224 | tf_op jit(solution)/shard_map/ppermute | solution.py:322
  36.9 1.6 %collective-permute-start.1 = (f32[256,256]{1,0:T(8,128)S(1)}, f32[256,256]{1,0:T(8,128)S(1)}, u32[]{:S(2)}, u32[]{:S(2)}) collective-permute-start(f32[256,256]{1,0:T(8,128)S(1)} %get-tuple-element.16), channel_id=1, source_target_pairs={{0,16},{16,0},{1,17},{17,1},{2,18},{18,2},{3,19},{19,3},{4,20},{20... | collective-permute-start | bytes 786440 | tf_op jit(solution)/shard_map/ppermute | solution.py:324

commit v4 on v3

--- a/solution.py
+++ b/solution.py
@@ -9,9 +9,7 @@
 BF16 = jnp.bfloat16
 F32 = jnp.float32
 NT = (((1,), (1,)), ((), ()))
-HEAD = 8
-HEAD_PARTS = 2
-REST_PARTS = 4
+PARTS = 7
 VMEM_SPEC = pl.BlockSpec(memory_space=pltpu.VMEM)
 HBM_SPEC = pl.BlockSpec(memory_space=pltpu.HBM)
 
@@ -37,11 +35,9 @@
     owner_hbm,
     energy_hbm,
     virt_hbm,
-    three_hbm,
     out_ref,
     info_ref,
     virt_ref,
-    head_ref,
     amp_ref,
     partner_ref,
     owner_ref,
@@ -54,10 +50,6 @@
     sources = (partner_hbm, owner_hbm, amp_hbm, energy_hbm, virt_hbm)
     targets = (partner_ref, owner_ref, amp_ref, energy_ref, virt_ref)
     copies = [pltpu.make_async_copy(a, b, sems.at[i]) for i, (a, b) in enumerate(zip(sources, targets))]
-    part = head_ref.shape[0] // HEAD_PARTS
-    for i in range(HEAD_PARTS):
-        rows = pl.ds(i * part, part)
-        copies.append(pltpu.make_async_copy(three_hbm.at[rows], head_ref.at[rows], sems.at[len(sources) + i]))
     for copy in copies:
         copy.start()
     count = partner_ref.shape[1]
@@ -102,30 +94,27 @@
     same = jnp.where(group >= jnp.broadcast_to(leaders, wide), 1.0, 0.0)
     info_ref[0] = jnp.where(iota(wide, 0) == 2, same, energies)
     info_ref[1] = jnp.broadcast_to(found, wide).astype(F32)
-    for copy in copies[len(sources) :]:
-        copy.wait()
-
-
-def plan(amplitudes, partner, owner, pair_energy, virt_energy, three_index, group, capacity):
+
+
+def plan(amplitudes, partner, owner, pair_energy, virt_energy, group, capacity):
     count, side, _ = amplitudes.shape
     virt = virt_energy.shape[0]
     amp = jnp.transpose(amplitudes, (1, 2, 0)).reshape(side * side, count)
     return pl.pallas_call(
         lambda *refs: plan_kernel(*refs, side=side, capacity=capacity),
-        in_specs=[VMEM_SPEC] + [HBM_SPEC] * 6,
-        out_specs=[VMEM_SPEC] * 4,
+        in_specs=[VMEM_SPEC] + [HBM_SPEC] * 5,
+        out_specs=[VMEM_SPEC] * 3,
         out_shape=[
             jax.ShapeDtypeStruct((count, side * side), BF16),
             jax.ShapeDtypeStruct((2, 8, 128), F32),
             jax.ShapeDtypeStruct((1, virt), F32),
-            jax.ShapeDtypeStruct((HEAD,) + three_index.shape[1:], BF16),
         ],
         scratch_shapes=[
             pltpu.VMEM((side * side, count), BF16),
             pltpu.VMEM((1, count), jnp.int32),
             pltpu.VMEM((1, count), jnp.int32),
             pltpu.VMEM((1, count), F32),
-            pltpu.SemaphoreType.DMA((5 + HEAD_PARTS,)),
+            pltpu.SemaphoreType.DMA((5,)),
         ],
         compiler_params=pltpu.CompilerParams(vmem_limit_bytes=8 << 20),
         name="plan",
@@ -136,19 +125,45 @@
         in_hbm(owner.reshape(1, count)),
         in_hbm(pair_energy.reshape(1, count)),
         in_hbm(virt_energy.reshape(1, virt)),
-        in_hbm(three_index),
     )
 
 
-def ladder_kernel(core_ref, info_ref, virt_ref, own_ref, other_ref, head_ref, three_hbm, keep_ref, send_ref, turned, rest_ref, sems, *, side):
-    virt = head_ref.shape[1]
-    head = head_ref.shape[0]
-    part = rest_ref.shape[0] // REST_PARTS
+def prep_kernel(info_ref, virt_ref, three_hbm, three_ref, scale_ref, sems):
+    part = three_ref.shape[0] // PARTS
     copies = []
-    for i in range(REST_PARTS):
-        source = three_hbm.at[pl.ds(head + i * part, part)]
-        copies.append(pltpu.make_async_copy(source, rest_ref.at[pl.ds(i * part, part)], sems.at[i]))
+    for i in range(PARTS):
+        rows = pl.ds(i * part, part)
+        copies.append(pltpu.make_async_copy(three_hbm.at[rows], three_ref.at[rows], sems.at[i]))
         copies[-1].start()
+    virt = virt_ref.shape[1]
+    rows_of = jnp.broadcast_to(virt_ref[...], (virt, virt))
+    sums = rows_of + rows_of.T
+    info = info_ref[0]
+    for slot in range(2):
+        scale_ref[slot] = 1.0 / (sums - info[slot : slot + 1, 0:1])
+    for copy in copies:
+        copy.wait()
+
+
+def prep(info, virt_row, three_index):
+    virt = three_index.shape[1]
+    return pl.pallas_call(
+        prep_kernel,
+        in_specs=[VMEM_SPEC] * 2 + [HBM_SPEC],
+        out_specs=[VMEM_SPEC] * 2,
+        out_shape=[
+            jax.ShapeDtypeStruct(three_index.shape, BF16),
+            jax.ShapeDtypeStruct((2, virt, virt), F32),
+        ],
+        scratch_shapes=[pltpu.SemaphoreType.DMA((PARTS,))],
+        compiler_params=pltpu.CompilerParams(vmem_limit_bytes=8 << 20),
+        cost_estimate=pl.CostEstimate(flops=0, bytes_accessed=2 * three_index.size, transcendentals=0),
+        name="prep",
+    )(info, virt_row, in_hbm(three_index))
+
+
+def ladder_kernel(core_ref, info_ref, scale_ref, own_ref, other_ref, b_ref, keep_ref, send_ref, turned, *, side):
+    naux, virt, _ = b_ref.shape
     half_lanes = virt // 2
     per_vector = half_lanes // side
     first_core = jnp.broadcast_to(core_ref[:1, :] == 0, (side, half_lanes))
@@ -190,30 +205,23 @@
             turned[rows, lanes] = vector[k * side : (k + 1) * side]
     amp_t = jnp.dot(swap_matrix(side), turned[...], preferred_element_type=F32).astype(BF16)
 
-    totals = [jnp.zeros((virt, virt), F32)] * 2
-    for i in range(REST_PARTS + 1):
-        if i == 0:
-            block_ref = head_ref
-        else:
-            copies[i - 1].wait()
-            block_ref = rest_ref.at[pl.ds((i - 1) * part, part)]
-        count = block_ref.shape[0]
-        rows = block_ref[...].reshape(count * virt, virt)
-        half = jnp.dot(rows, amp_t, preferred_element_type=F32).astype(BF16)
-        for slot in range(2):
-            for q in range(count):
-                totals[slot] = totals[slot] + lax.dot_general(
-                    half[q * virt : (q + 1) * virt, slot * virt : (slot + 1) * virt],
-                    block_ref[q],
-                    NT,
-                    preferred_element_type=F32,
-                )
-
-    rows_of = jnp.broadcast_to(virt_ref[...], (virt, virt))
-    sums = rows_of + rows_of.T
+    rows = b_ref[...].reshape(naux * virt, virt)
+    half = jnp.dot(rows, amp_t, preferred_element_type=F32).astype(BF16)
+    totals = []
+    for slot in range(2):
+        total = jnp.zeros((virt, virt), F32)
+        for q in range(naux):
+            total += lax.dot_general(
+                half[q * virt : (q + 1) * virt, slot * virt : (slot + 1) * virt],
+                b_ref[q],
+                NT,
+                preferred_element_type=F32,
+            )
+        totals.append(total)
+
     info = info_ref[0]
-    first = totals[0] / (sums - info[0:1, 0:1])
-    second = totals[1] / (sums - info[1:2, 0:1])
+    first = totals[0] * scale_ref[0]
+    second = totals[1] * scale_ref[1]
     same = jnp.broadcast_to(info[2:3, 0:1] > 0.5, (virt, virt))
     blocks = (first.T + jnp.where(same, first, second), second.T + jnp.where(same, second, first))
     on_first = jnp.broadcast_to(core_ref[:1, :1] == 0, (virt, virt))
@@ -221,28 +229,23 @@
     send_ref[...] = jnp.where(on_first, blocks[1], blocks[0])
 
 
-def ladder(core, info, virt_row, own, other, head, three_index, side):
-    naux, virt, _ = three_index.shape
+def ladder(core, info, scale, own, other, three, side):
+    _, virt, _ = three.shape
     return pl.pallas_call(
         lambda *refs: ladder_kernel(*refs, side=side),
-        in_specs=[VMEM_SPEC] * 6 + [HBM_SPEC],
+        in_specs=[VMEM_SPEC] * 6,
         out_specs=[VMEM_SPEC] * 2,
         out_shape=[jax.ShapeDtypeStruct((virt, virt), F32)] * 2,
-        scratch_shapes=[
-            pltpu.VMEM((virt, 2 * virt), BF16),
-            pltpu.VMEM((naux - HEAD, virt, virt), BF16),
-            pltpu.SemaphoreType.DMA((REST_PARTS,)),
-        ],
+        scratch_shapes=[pltpu.VMEM((virt, 2 * virt), BF16)],
         compiler_params=pltpu.CompilerParams(vmem_limit_bytes=40 << 20),
         name="ladder",
     )(
         jnp.full((8, 128), core, jnp.int32),
         info,
-        virt_row,
+        scale,
         own,
         other,
-        head,
-        in_hbm(three_index),
+        three,
     )
 
 
@@ -311,16 +314,17 @@
     pairs_all, side, _ = amplitudes.shape
     virt = three_index.shape[1]
     capacity = 2 * (pairs_all // groups)
-    tiles, info, virt_row, head = plan(
-        amplitudes, partner, owner, pair_energy, virt_energy, three_index, lax.axis_index("pairs"), capacity
+    tiles, info, virt_row = plan(
+        amplitudes, partner, owner, pair_energy, virt_energy, lax.axis_index("pairs"), capacity
     )
     outgoing = jnp.broadcast_to(
         tiles.reshape(1, groups, 2, side * side), (depth, groups, 2, side * side)
     ).reshape(depth * groups, 2, side * side)
     arrived = lax.all_to_all(outgoing, ("z", "pairs"), split_axis=0, concat_axis=0, tiled=True)
+    three, scale = prep(info, virt_row, three_index)
     own = jnp.transpose(arrived, (1, 0, 2))
     other = lax.ppermute(own, "core", swap)
-    keep, send = ladder(core, info, virt_row, own, other, head, three_index, side)
+    keep, send = ladder(core, info, scale, own, other, three, side)
     partial = merge(keep, lax.ppermute(send, "core", swap), aux)
     shares = lax.all_to_all(partial, aux_axes, split_axis=0, concat_axis=0, tiled=True)
     spread = gather(shares, groups)

time: 62.5 us -> 63.3 us (1.013)
  Pallas kernels: 6.91 us -> 8.87 us
  waiting for transfers between devices: 2.16 us -> 1.52 us
    pallas_call x0 -> x1, Pallas kernels: none -> 2.06 us  [prep(): pl.pallas_call(prep_kernel, in_specs=[VMEM_SPEC] * 2 + [HBM_SPEC], out_sp...]
    ppermute x1, waiting for transfers between devices: 0.99 us -> 0.01 us  [per_device(): other = lax.ppermute(own, 'core', swap)]
  transfers between devices with their start and end apart: 2 -> 2, of which waited for: 2 -> 1; matrix products, arithmetic and copies ran while one was open for 0% -> 0% of each run, Pallas kernels for 0% -> 3%
where the time goes in v4:
time: 63.3 us; the launch traced here: 63 us
  blocking collectives  50.2 us (79%)
  Pallas kernels  8.87 us (14%)
  starting transfers between devices  2.3 us (4%)
  waiting for transfers between devices  1.52 us (2%)
    all_to_all x1, blocking collectives, per_device(): lax.all_to_all(outgoing, ('z', 'pairs'), split_axis=0, concat_axis=0, til...  27.4 us
    all_to_all x1, blocking collectives, per_device(): lax.all_to_all(partial, aux_axes, split_axis=0, concat_axis=0, tiled=True)  11.7 us
    all_to_all x1, blocking collectives, per_device(): lax.all_to_all(spread, 'pairs', split_axis=0, concat_axis=0, tiled=True)  11.1 us
    pallas_call x1, Pallas kernels, ladder(): pl.pallas_call(lambda *refs: ladder_kernel(*refs, side=side), in_specs=[V...  4.78 us
    ppermute x1, starting transfers between devices, per_device(): other = lax.ppermute(own, 'core', swap)  2.19 us
    pallas_call x1, Pallas kernels, prep(): pl.pallas_call(prep_kernel, in_specs=[VMEM_SPEC] * 2 + [HBM_SPEC], out_sp...  2.06 us
    ppermute x1, waiting for transfers between devices, per_device(): partial = merge(keep, lax.ppermute(send, 'core', swap), aux)  1.51 us
    pallas_call x1, Pallas kernels, plan(): pl.pallas_call(lambda *refs: plan_kernel(*refs, side=side, capacity=capac...  1.28 us
  transfers between devices with their start and end apart: 2, of which 1 were waited for; matrix products, arithmetic and copies ran while one was open for 0% of the time, Pallas kernels for 3%

profile of v4, /device:TPU:1, one launch (start us, length us, event | category | flops | bytes accessed | tf_op | source)
XLA Modules:
  0.0 63.0 jit_solution(7795811822681599046)
XLA Ops:
  0.0 1.3 %plan.1 = (bf16[32,256]{1,0:T(8,128)(2,1)S(1)}, f32[2,8,128]{2,1,0:T(8,128)S(1)}, f32[1,256]{1,0:T(1,128)S(1)}) custom-call(s32[8,128]{1,0:T(8,128)S(1)} %broadcast_in_dim.13.refs_0_, bf16[256,32]{1,0:T(8,128)(2,1)} %bitcast.16, s32[1,32]{1,0:T(1,128)} %bitcast.18, s32[1,32]{1,0:T(1,128)} %bitcast.19, f32[1,32]{1,0:T(1,128)} %bitcast.20, f32[1,256]{1,0:T(1,128)} %bitcast.17), custom_call_target="tpu_custom_call" | custom-call | tf_op jit(solution)/shard_map/plan/pallas_call | solution.py:103
  1.3 0.1 broadcast_in_dim.16
  1.4 27.4 %all_to_all.15 = bf16[128,2,256]{2,1,0:T(2,128)(2,1)S(1)} all-to-all(bf16[128,2,256]{2,1,0:T(2,128)(2,1)S(1)} %bitcast.15), channel_id=1, replica_groups=mesh['z'=8,'core'=2,'pairs'=16] {'z','pairs'}, dimensions={0} | all-to-all | bytes 262144 | tf_op jit(solution)/shard_map/all_to_all | solution.py:323
  28.8 2.2 %collective-permute-start = (bf16[2,128,256]{2,1,0:T(8,128)(2,1)S(1)}, bf16[2,128,256]{2,1,0:T(8,128)(2,1)S(1)}, u32[]{:S(2)}, u32[]{:S(2)}) collective-permute-start(bf16[2,128,256]{2,1,0:T(8,128)(2,1)S(1)} %bitcast.13), channel_id=1, source_target_pairs={{0,16},{16,0},{1,17},{17,1},{2,18},{18,2},{3,19},{19,3},{4,20},{20... | collective-permute-start | bytes 393224 | tf_op jit(solution)/shard_map/ppermute | solution.py:326
  31.0 2.1 %prep.1 = (bf16[28,256,256]{2,1,0:T(8,128)(2,1)S(1)}, f32[2,256,256]{2,1,0:T(8,128)S(1)}) custom-call(f32[2,8,128]{2,1,0:T(8,128)S(1)} %get-tuple-element.12.info_ref.refs_1_, f32[1,256]{1,0:T(1,128)S(1)} %get-tuple-element.13.virt_ref, bf16[28,256,256]{2,1,0:T(8,128)(2,1)} %three_hbm.1), custom_call_target="tpu_custom_call" | custom-call | bytes 3670016 | tf_op jit(solution)/shard_map/prep/pallas_call | solution.py:150
  33.0 0.0 collective-permute-done.refs_4_
  33.1 4.8 %ladder.1 = (f32[256,256]{1,0:T(8,128)S(1)}, f32[256,256]{1,0:T(8,128)S(1)}) custom-call(s32[8,128]{1,0:T(8,128)S(1)} %broadcast_in_dim.14.refs_0_, f32[2,8,128]{2,1,0:T(8,128)S(1)} %get-tuple-element.12.info_ref.refs_1_, f32[2,256,256]{2,1,0:T(8,128)S(1)} %get-tuple-element.14.refs_2_, bf16[2,128,256]{2,1,0:T(8,128)(2,1)S(1)} %bitcast.14, ...), custom_call_target="tpu_custom_call" | custom-call | tf_op jit(solution)/shard_map/ladder/pallas_call | solution.py:234
  37.8 0.1 collective-permute-start.1
  37.9 1.5 %collective-permute-done.1.came_ref = f32[256,256]{1,0:T(8,128)S(1)} collective-permute-done((f32[256,256]{1,0:T(8,128)S(1)}, f32[256,256]{1,0:T(8,128)S(1)}, u32[]{:S(2)}, u32[]{:S(2)}) %collective-permute-start.1) | collective-permute-done | bytes 262176 | tf_op jit(solution)/shard_map/ppermute | solution.py:328
  39.5 11.7 %all_to_all.16.shares_ref = bf16[16,16,256]{2,1,0:T(8,128)(2,1)S(1)} all-to-all(bf16[16,16,256]{2,1,0:T(8,128)(2,1)S(1)} %merge.1), channel_id=1, replica_groups=mesh['z'=8,'core'=2,'pairs'=16] {'z','core'}, dimensions={0} | all-to-all | bytes 262144 | tf_op jit(solution)/shard_map/all_to_all | solution.py:329
  51.3 11.1 %all_to_all.17 = bf16[16,2,16,256]{3,2,1,0:T(8,128)(2,1)S(1)} all-to-all(bf16[16,2,16,256]{3,2,1,0:T(8,128)(2,1)S(1)} %gather.1), channel_id=1, replica_groups=mesh['z'=8,'core'=2,'pairs'=16] {'pairs'}, dimensions={0} | all-to-all | bytes 524288 | tf_op jit(solution)/shard_map/all_to_all | solution.py:331
  62.4 0.7 %select.1 = f32[4,16,256]{2,1,0:T(8,128)} custom-call(f32[2,8,128]{2,1,0:T(8,128)S(1)} %get-tuple-element.12.info_ref.refs_1_, bf16[32,16,256]{2,1,0:T(8,128)(2,1)S(1)} %bitcast.12), custom_call_target="tpu_custom_call" | custom-call | tf_op jit(solution)/shard_map/select/pallas_call | solution.py:297
  (6 shorter events, 0.1 us)
Async XLA Ops:
  28.8 4.3 %collective-permute-start = (bf16[2,128,256]{2,1,0:T(8,128)(2,1)S(1)}, bf16[2,128,256]{2,1,0:T(8,128)(2,1)S(1)}, u32[]{:S(2)}, u32[]{:S(2)}) collective-permute-start(bf16[2,128,256]{2,1,0:T(8,128)(2,1)S(1)} %bitcast.13), channel_id=1, source_target_pairs={{0,16},{16,0},{1,17},{17,1},{2,18},{18,2},{3,19},{19,3},{4,20},{20... | collective-permute-start | bytes 393224 | tf_op jit(solution)/shard_map/ppermute | solution.py:326
  37.8 1.6 %collective-permute-start.1 = (f32[256,256]{1,0:T(8,128)S(1)}, f32[256,256]{1,0:T(8,128)S(1)}, u32[]{:S(2)}, u32[]{:S(2)}) collective-permute-start(f32[256,256]{1,0:T(8,128)S(1)} %get-tuple-element.18), channel_id=1, source_target_pairs={{0,16},{16,0},{1,17},{17,1},{2,18},{18,2},{3,19},{19,3},{4,20},{20... | collective-permute-start | bytes 786440 | tf_op jit(solution)/shard_map/ppermute | solution.py:328

commit v5 on v3

v5 whole, which is shorter than its diff:
```python
import jax
import jax.numpy as jnp
from jax import lax
from jax.experimental import pallas as pl
from jax.experimental.pallas import tpu as pltpu
from jax.sharding import Mesh
from jax.sharding import PartitionSpec as P


BF16 = jnp.bfloat16
F32 = jnp.float32
NT = (((1,), (1,)), ((), ()))
HEAD = 8
HEAD_PARTS = 2
OWN_PARTS = 4
OTHER_PARTS = 4
VMEM_SPEC = pl.BlockSpec(memory_space=pltpu.VMEM)
HBM_SPEC = pl.BlockSpec(memory_space=pltpu.HBM)


def in_hbm(x):
    return pltpu.with_memory_space_constraint(x, pltpu.HBM)


def iota(shape, dim):
    return lax.broadcasted_iota(jnp.int32, shape, dim)


def swap_matrix(side):
    full = side * side
    turned = (iota((full, full), 0) % side) * side + iota((full, full), 0) // side
    return jnp.where(turned == iota((full, full), 1), 1.0, 0.0).astype(BF16)


def plan_kernel(
    group_ref,
    core_ref,
    amp_hbm,
    partner_hbm,
    owner_hbm,
    energy_hbm,
    virt_hbm,
    three_hbm,
    pick_ref,
    info_ref,
    virt_ref,
    amp_ref,
    head_ref,
    partner_ref,
    owner_ref,
    energy_ref,
    sems,
    *,
    capacity,
):
    sources = (partner_hbm, owner_hbm, energy_hbm, virt_hbm, amp_hbm)
    targets = (partner_ref, owner_ref, energy_ref, virt_ref, amp_ref)
    copies = [pltpu.make_async_copy(a, b, sems.at[i]) for i, (a, b) in enumerate(zip(sources, targets))]
    part = head_ref.shape[0] // HEAD_PARTS
    for i in range(HEAD_PARTS):
        rows = pl.ds(i * part, part)
        copies.append(pltpu.make_async_copy(three_hbm.at[rows], head_ref.at[rows], sems.at[len(sources) + i]))
    for copy in copies:
        copy.start()
    count = partner_ref.shape[1]
    square = (count, count)
    group = group_ref[...]
    core = core_ref[...]
    row = iota(square, 0)
    col = iota(square, 1)
    diagonal = row == col
    for copy in copies[:3]:
        copy.wait()
    partner = jnp.broadcast_to(partner_ref[...], square)
    owner = jnp.broadcast_to(owner_ref[...], square)

    def down(x):
        return jnp.sum(jnp.where(diagonal, x, 0), axis=1, keepdims=True)

    leads = (partner > col).astype(jnp.int32)
    fixed = (partner == col).astype(jnp.int32)
    low = jnp.minimum(partner, col)
    lead_rank = jnp.sum(jnp.where(row < low, down(leads), 0), axis=0, keepdims=True)
    fixed_rank = jnp.sum(jnp.where(row < col, down(fixed), 0), axis=0, keepdims=True)
    leaders = jnp.sum(leads[:1], axis=1, keepdims=True)
    late = (col[:1] > partner[:1]).astype(jnp.int32)
    place = jnp.where(fixed[:1] > 0, 2 * leaders + fixed_rank, 2 * lead_rank + late)
    slot = row - row % 2 + jnp.broadcast_to(core[:1, :count], square)
    hit = jnp.broadcast_to(place, square) == slot
    for which in range(2):
        pick_ref[which] = jnp.where(hit & (row % 2 == which), 1.0, 0.0).astype(BF16)
    slot_rank = jnp.sum(((down(owner) == owner) & (row < col)).astype(jnp.int32), axis=0, keepdims=True)
    position = owner_ref[...] * capacity + slot_rank
    small = (8, count)
    wide = (8, 128)
    my_group = jnp.broadcast_to(group[:1, :count], small)
    my_core = jnp.broadcast_to(core[:1, :count], small)
    mine = jnp.broadcast_to(position, small) == iota(small, 0) + capacity * my_group
    found = jnp.sum(jnp.where(mine, jnp.broadcast_to(place + 1, small), 0), axis=1, keepdims=True)
    chosen = jnp.broadcast_to(place, small) == 2 * my_group + my_core
    energy = jnp.sum(jnp.where(chosen, jnp.broadcast_to(energy_ref[...], small), 0.0), axis=1, keepdims=True)
    same = jnp.where(group >= jnp.broadcast_to(leaders, wide), 1.0, 0.0)
    info_ref[0] = jnp.where(iota(wide, 0) == 2, same, jnp.broadcast_to(energy, wide))
    info_ref[1] = jnp.broadcast_to(found, wide).astype(F32)
    for copy in copies[3:]:
        copy.wait()


def plan(amp, partner, owner, pair_energy, virt_energy, three_index, group, core, capacity):
    count = partner.shape[0]
    virt = virt_energy.shape[0]
    return pl.pallas_call(
        lambda *refs: plan_kernel(*refs, capacity=capacity),
        in_specs=[VMEM_SPEC] * 2 + [HBM_SPEC] * 6,
        out_specs=[VMEM_SPEC] * 5,
        out_shape=[
            jax.ShapeDtypeStruct((2, count, count), BF16),
            jax.ShapeDtypeStruct((2, 8, 128), F32),
            jax.ShapeDtypeStruct((1, virt), F32),
            jax.ShapeDtypeStruct(amp.shape, BF16),
            jax.ShapeDtypeStruct((HEAD,) + three_index.shape[1:], BF16),
        ],
        scratch_shapes=[
            pltpu.VMEM((1, count), jnp.int32),
            pltpu.VMEM((1, count), jnp.int32),
            pltpu.VMEM((1, count), F32),
            pltpu.SemaphoreType.DMA((5 + HEAD_PARTS,)),
        ],
        compiler_params=pltpu.CompilerParams(vmem_limit_bytes=8 << 20),
        cost_estimate=pl.CostEstimate(flops=0, bytes_accessed=2 << 20, transcendentals=0),
        name="plan",
    )(
        jnp.full((8, 128), group, jnp.int32),
        jnp.full((8, 128), core, jnp.int32),
        in_hbm(amp),
        in_hbm(partner.reshape(1, count)),
        in_hbm(owner.reshape(1, count)),
        in_hbm(pair_energy.reshape(1, count)),
        in_hbm(virt_energy.reshape(1, virt)),
        in_hbm(three_index),
    )


def pack_kernel(pick_ref, own_ref, other_ref, out_ref, *, side):
    tiles = lax.dot_general(pick_ref[0], own_ref[...], NT, preferred_element_type=F32)
    tiles += lax.dot_general(pick_ref[1], other_ref[...], NT, preferred_element_type=F32)
    out_ref[...] = jnp.dot(tiles.astype(BF16), swap_matrix(side), preferred_element_type=F32).astype(BF16)


def pack(pick, own, other, side):
    return pl.pallas_call(
        lambda *refs: pack_kernel(*refs, side=side),
        in_specs=[VMEM_SPEC] * 3,
        out_specs=VMEM_SPEC,
        out_shape=jax.ShapeDtypeStruct((pick.shape[1], own.shape[0]), BF16),
        compiler_params=pltpu.CompilerParams(vmem_limit_bytes=8 << 20),
        name="pack",
    )(pick, own, other)


def ladder_kernel(
    core_ref, info_ref, virt_ref, tiles_ref, head_ref, own_hbm, other_hbm, out_ref, turned, own_ref, other_ref, sems, *, side
):
    head, virt, _ = head_ref.shape
    copies = []
    blocks = [head_ref]
    for source, target, skip, parts in ((own_hbm, own_ref, head, OWN_PARTS), (other_hbm, other_ref, 0, OTHER_PARTS)):
        part = target.shape[0] // parts
        for i in range(parts):
            block = target.at[pl.ds(i * part, part)]
            copy = pltpu.make_async_copy(source.at[pl.ds(skip + i * part, part)], block, sems.at[len(copies)])
            copy.start()
            copies.append(copy)
            blocks.append(block)
    half_lanes = virt // 2
    per_vector = half_lanes // side
    first_core = jnp.broadcast_to(core_ref[:1, :] == 0, (side, half_lanes))

    def piece(z, core, half):
        rows = pl.ds(z * side, side)
        lanes = pl.ds(half * half_lanes, half_lanes)
        own = tiles_ref[0, rows, lanes]
        other = tiles_ref[1, rows, lanes]
        return jnp.where(first_core, own, other) if core == 0 else jnp.where(first_core, other, own)

    order = [(half, high) for half in range(2) for high in range(2)]
    vectors = []
    for low in range(per_vector):
        z_low, core = low // 2, low % 2
        vectors.append(
            jnp.concatenate([piece(high * (per_vector // 2) + z_low, core, half) for half, high in order], axis=0)
        )
    lane_group = iota(vectors[0].shape, 1) // side
    step = 1
    while step < per_vector:
        keep = (lane_group & step) == 0
        shift = step * side
        for i in range(per_vector):
            if i & step:
                continue
            j = i | step
            a, b = vectors[i], vectors[j]
            vectors[i] = jnp.where(keep, a, pltpu.roll(b, shift, 1))
            vectors[j] = jnp.where(keep, pltpu.roll(a, half_lanes - shift, 1), b)
        step *= 2
    for s_low in range(per_vector):
        for k, (half, high) in enumerate(order):
            rows = pl.ds((half * per_vector + s_low) * side, side)
            lanes = pl.ds(high * half_lanes, half_lanes)
            turned[rows, lanes] = vectors[s_low][k * side : (k + 1) * side]
    amp_t = jnp.dot(swap_matrix(side), turned[...], preferred_element_type=F32).astype(BF16)

    total = jnp.zeros((virt, virt), F32)
    for i, block in enumerate(blocks):
        if i > 0:
            copies[i - 1].wait()
        count = block.shape[0]
        rows = block[...].reshape(count * virt, virt)
        product = jnp.dot(rows, amp_t, preferred_element_type=F32).astype(BF16)
        for q in range(count):
            total += lax.dot_general(
                product[q * virt : (q + 1) * virt], block[q], NT, preferred_element_type=F32
            )

    rows_of = jnp.broadcast_to(virt_ref[...], (virt, virt))
    out_ref[...] = total / (rows_of + rows_of.T - info_ref[0, 0:1, 0:1])


def ladder(core, info, virt_row, tiles, head, three_index, three_other, side):
    naux, virt, _ = three_index.shape
    return pl.pallas_call(
        lambda *refs: ladder_kernel(*refs, side=side),
        in_specs=[VMEM_SPEC] * 5 + [HBM_SPEC] * 2,
        out_specs=VMEM_SPEC,
        out_shape=jax.ShapeDtypeStruct((virt, virt), F32),
        scratch_shapes=[
            pltpu.VMEM((virt, virt), BF16),
            pltpu.VMEM((naux - HEAD, virt, virt), BF16),
            pltpu.VMEM((naux, virt, virt), BF16),
            pltpu.SemaphoreType.DMA((OWN_PARTS + OTHER_PARTS,)),
        ],
        compiler_params=pltpu.CompilerParams(vmem_limit_bytes=40 << 20),
        name="ladder",
    )(
        jnp.full((8, 128), core, jnp.int32),
        info,
        virt_row,
        tiles,
        head,
        in_hbm(three_index),
        in_hbm(three_other),
    )


def merge_kernel(info_ref, own_ref, other_ref, out_ref):
    own = own_ref[...]
    same = jnp.broadcast_to(info_ref[0, 2:3, 0:1] > 0.5, own.shape)
    total = own.T + jnp.where(same, own, other_ref[...])
    out_ref[...] = total.astype(BF16).reshape(out_ref.shape)


def merge(info, own, other, aux):
    virt = own.shape[0]
    return pl.pallas_call(
        merge_kernel,
        in_specs=[VMEM_SPEC] * 3,
        out_specs=VMEM_SPEC,
        out_shape=jax.ShapeDtypeStruct((aux, virt // aux, virt), BF16),
        compiler_params=pltpu.CompilerParams(vmem_limit_bytes=8 << 20),
        name="merge",
    )(info, own, other)


def gather_kernel(shares_ref, out_ref):
    for core in range(2):
        total = shares_ref[core].astype(F32)
        for k in range(core + 2, shares_ref.shape[0], 2):
            total += shares_ref[k].astype(F32)
        done = total.astype(BF16)
        for k in range(out_ref.shape[0]):
            out_ref[k, core] = done


def gather(shares, groups):
    return pl.pallas_call(
        gather_kernel,
        in_specs=[VMEM_SPEC],
        out_specs=VMEM_SPEC,
        out_shape=jax.ShapeDtypeStruct((groups, 2) + shares.shape[1:], BF16),
        compiler_params=pltpu.CompilerParams(vmem_limit_bytes=8 << 20),
        name="gather",
    )(shares)


def select_kernel(info_ref, found_ref, out_ref):
    for k in range(out_ref.shape[0]):
        index = info_ref[1, k, 0].astype(jnp.int32)
        block = found_ref[jnp.maximum(index - 1, 0)].astype(F32)
        out_ref[k] = jnp.where(index > 0, block, 0.0)


def select(info, found, capacity):
    return pl.pallas_call(
        select_kernel,
        in_specs=[VMEM_SPEC] * 2,
        out_specs=VMEM_SPEC,
        out_shape=jax.ShapeDtypeStruct((capacity,) + found.shape[1:], F32),
        compiler_params=pltpu.CompilerParams(vmem_limit_bytes=8 << 20),
        name="select",
    )(info, found)


def per_device(amplitudes, three_index, virt_energy, pair_energy, owner, partner):
    aux_axes = ("z", "core")
    swap = [(0, 1), (1, 0)]
    aux = lax.axis_size(aux_axes)
    depth = lax.axis_size("z")
    groups = lax.axis_size("pairs")
    core = lax.axis_index("core")
    pairs_all, side, _ = amplitudes.shape
    virt = three_index.shape[1]
    capacity = 2 * (pairs_all // groups)
    amp = jnp.transpose(amplitudes, (1, 2, 0)).reshape(side * side, pairs_all)
    amp_other = lax.ppermute(amp, "core", swap)
    pick, info, virt_row, amp_own, head = plan(
        amp, partner, owner, pair_energy, virt_energy, three_index, lax.axis_index("pairs"), core, capacity
    )
    three_late, amp_other = lax.optimization_barrier((three_index, amp_other))
    three_other = lax.ppermute(three_late, "core", swap)
    tiles = pack(pick, amp_own, amp_other, side)
    outgoing = jnp.broadcast_to(
        tiles.reshape(1, groups, 2, side * side), (depth, groups, 2, side * side)
    ).reshape(depth * groups, 2, side * side)
    arrived = lax.all_to_all(outgoing, ("z", "pairs"), split_axis=0, concat_axis=0, tiled=True)
    arrived = jnp.transpose(arrived, (1, 0, 2))
    turned = ladder(core, info, virt_row, arrived, head, three_index, three_other, side)
    partial = merge(info, turned, lax.ppermute(turned, "core", swap), aux)
    shares = lax.all_to_all(partial, aux_axes, split_axis=0, concat_axis=0, tiled=True)
    spread = gather(shares, groups)
    found = lax.all_to_all(spread, "pairs", split_axis=0, concat_axis=0, tiled=True)
    return select(info, found.reshape(pairs_all, side, virt), capacity)


def solution(mesh):
    groups = mesh.shape["pairs"]
    devices = mesh.devices.reshape(mesh.shape["aux"] // 2, 2, groups)
    split = Mesh(devices, ("z", "core", "pairs"))
    aux = ("z", "core")
    placed = (P(None, aux, "pairs"), P(aux, None, None), P(), P(), P(), P())
    return jax.shard_map(
        per_device, mesh=split, in_specs=placed, out_specs=P("pairs", aux, None), check_vma=False
    )
```

time: 62.5 us -> 65.6 us (1.050)
  starting transfers between devices: 2.64 us -> 5.53 us
  Pallas kernels: 6.91 us -> 9.27 us
  blocking collectives: 50.4 us -> 48.1 us
    ppermute x2 -> x3, starting transfers between devices: 2.64 us -> 5.53 us  [the longest x1 3.2 us: per_device(): amp_other = lax.ppermute(amp, 'core', swap)]
    all_to_all x1, blocking collectives: 27.4 us -> 25 us  [per_device(): lax.all_to_all(outgoing, ('z', 'pairs'), split_axis=0, concat_axis=0, til...]
    pallas_call x1, Pallas kernels: 4.81 us -> 6.77 us  [ladder(): pl.pallas_call(lambda *refs: ladder_kernel(*refs, side=side), in_specs=[V...]
    pallas_call x2 -> x3, Pallas kernels: 1.39 us -> 1.79 us  [the longest x1 1.36 us: plan(): pl.pallas_call(lambda *refs: plan_kernel(*refs, capacity=capacity), in_sp...]
    ppermute x2 -> x3, waiting for transfers between devices: 2.16 us -> 2.28 us  [the longest x1 1.16 us: per_device(): partial = merge(info, turned, lax.ppermute(turned, 'core', swap), aux)]
  transfers between devices with their start and end apart: 2 -> 3, of which waited for: 2 -> 2; matrix products, arithmetic and copies ran while one was open for 0% -> 0% of each run, Pallas kernels for 0% -> 3%
where the time goes in v5:
time: 65.6 us; the launch traced here: 65.3 us
  blocking collectives  48.1 us (73%)
  Pallas kernels  9.27 us (14%)
  starting transfers between devices  5.53 us (8%)
  waiting for transfers between devices  2.28 us (3%)
    all_to_all x1, blocking collectives, per_device(): lax.all_to_all(outgoing, ('z', 'pairs'), split_axis=0, concat_axis=0, til...  25 us
    all_to_all x1, blocking collectives, per_device(): lax.all_to_all(partial, aux_axes, split_axis=0, concat_axis=0, tiled=True)  12 us
    all_to_all x1, blocking collectives, per_device(): lax.all_to_all(spread, 'pairs', split_axis=0, concat_axis=0, tiled=True)  11.1 us
    pallas_call x1, Pallas kernels, ladder(): pl.pallas_call(lambda *refs: ladder_kernel(*refs, side=side), in_specs=[V...  6.77 us
    ppermute x1, starting transfers between devices, per_device(): amp_other = lax.ppermute(amp, 'core', swap)  3.2 us
    ppermute x1, starting transfers between devices, per_device(): partial = merge(info, turned, lax.ppermute(turned, 'core', swap), aux)  1.98 us
    pallas_call x1, Pallas kernels, plan(): pl.pallas_call(lambda *refs: plan_kernel(*refs, capacity=capacity), in_sp...  1.36 us
  transfers between devices with their start and end apart: 3, of which 2 were waited for; matrix products, arithmetic and copies ran while one was open for 0% of the time, Pallas kernels for 3%

profile of v5, /device:TPU:1, one launch (start us, length us, event | category | flops | bytes accessed | tf_op | source)
XLA Modules:
  0.0 65.3 jit_solution(16271984627764046803)
XLA Ops:
  0.0 3.2 %collective-permute-start = (bf16[256,32]{1,0:T(8,128)(2,1)}, bf16[256,32]{1,0:T(8,128)(2,1)S(1)}, u32[]{:S(2)}, u32[]{:S(2)}) collective-permute-start(bf16[256,32]{1,0:T(8,128)(2,1)} %bitcast.15), channel_id=1, source_target_pairs={{0,16},{16,0},{1,17},{17,1},{2,18},{18,2},{3,19},{19,3},{4,20},{20... | collective-permute-start | bytes 49160 | tf_op jit(solution)/shard_map/ppermute | solution.py:324
  3.2 1.1 %collective-permute-done.refs_2_ = bf16[256,32]{1,0:T(8,128)(2,1)S(1)} collective-permute-done((bf16[256,32]{1,0:T(8,128)(2,1)}, bf16[256,32]{1,0:T(8,128)(2,1)S(1)}, u32[]{:S(2)}, u32[]{:S(2)}) %collective-permute-start) | collective-permute-done | bytes 16416 | tf_op jit(solution)/shard_map/ppermute | solution.py:324
  4.3 0.4 collective-permute-start.1
  4.7 1.4 %plan.1 = (bf16[2,32,32]{2,1,0:T(8,128)(2,1)S(1)}, f32[2,8,128]{2,1,0:T(8,128)S(1)}, f32[1,256]{1,0:T(1,128)S(1)}, bf16[256,32]{1,0:T(8,128)(2,1)S(1)}, bf16[8,256,256]{2,1,0:T(8,128)(2,1)S(1)}) custom-call(s32[8,128]{1,0:T(8,128)S(1)} %broadcast_in_dim.14.refs_0_, s32[8,128]{1,0:T(8,128)S(1)} %broadcast_in_dim.15.refs_1_.refs_0_, bf16[256,32]{1,0:T(8,128)(2,1)} %bitcast.16, ...), custom_call_target="tpu_custom_call" | custom-call | bytes 2097152 | tf_op jit(solution)/shard_map/plan/pallas_call | solution.py:112
  6.0 0.3 pack.1
  6.4 0.1 broadcast_in_dim.17
  6.4 25.0 %all_to_all.15 = bf16[128,2,256]{2,1,0:T(2,128)(2,1)S(1)} all-to-all(bf16[128,2,256]{2,1,0:T(2,128)(2,1)S(1)} %bitcast.14), channel_id=1, replica_groups=mesh['z'=8,'core'=2,'pairs'=16] {'z','pairs'}, dimensions={0} | all-to-all | bytes 262144 | tf_op jit(solution)/shard_map/all_to_all | solution.py:334
  31.5 0.0 collective-permute-done.1.refs_6_
  31.5 6.8 %ladder.1.own_ref = f32[256,256]{1,0:T(8,128)S(1)} custom-call(s32[8,128]{1,0:T(8,128)S(1)} %broadcast_in_dim.15.refs_1_.refs_0_, f32[2,8,128]{2,1,0:T(8,128)S(1)} %get-tuple-element.12.refs_1_.info_ref, f32[1,256]{1,0:T(1,128)S(1)} %get-tuple-element.13.refs_2_, bf16[2,128,256]{2,1,0:T(8,128)(2,1)S(1)} %bitcast.13, ...), custom_call_target="tpu_custom_call" | custom-call | tf_op jit(solution)/shard_map/ladder/pallas_call | solution.py:231
  38.3 2.0 %collective-permute-start.2 = (f32[256,256]{1,0:T(8,128)S(1)}, f32[256,256]{1,0:T(8,128)S(1)}, u32[]{:S(2)}, u32[]{:S(2)}) collective-permute-start(f32[256,256]{1,0:T(8,128)S(1)} %ladder.1.own_ref), channel_id=1, source_target_pairs={{0,16},{16,0},{1,17},{17,1},{2,18},{18,2},{3,19},{19,3},{4,20},{20... | collective-permute-start | bytes 786440 | tf_op jit(solution)/shard_map/ppermute | solution.py:337
  40.3 1.2 %collective-permute-done.2.other_ref = f32[256,256]{1,0:T(8,128)S(1)} collective-permute-done((f32[256,256]{1,0:T(8,128)S(1)}, f32[256,256]{1,0:T(8,128)S(1)}, u32[]{:S(2)}, u32[]{:S(2)}) %collective-permute-start.2) | collective-permute-done | bytes 262176 | tf_op jit(solution)/shard_map/ppermute | solution.py:337
  41.4 0.1 merge.1
  41.6 12.0 %all_to_all.16.shares_ref = bf16[16,16,256]{2,1,0:T(8,128)(2,1)S(1)} all-to-all(bf16[16,16,256]{2,1,0:T(8,128)(2,1)S(1)} %merge.1), channel_id=1, replica_groups=mesh['z'=8,'core'=2,'pairs'=16] {'z','core'}, dimensions={0} | all-to-all | bytes 262144 | tf_op jit(solution)/shard_map/all_to_all | solution.py:338
  53.6 11.1 %all_to_all.17 = bf16[16,2,16,256]{3,2,1,0:T(8,128)(2,1)S(1)} all-to-all(bf16[16,2,16,256]{3,2,1,0:T(8,128)(2,1)S(1)} %gather.1), channel_id=1, replica_groups=mesh['z'=8,'core'=2,'pairs'=16] {'pairs'}, dimensions={0} | all-to-all | bytes 524288 | tf_op jit(solution)/shard_map/all_to_all | solution.py:340
  64.7 0.7 %select.1 = f32[4,16,256]{2,1,0:T(8,128)} custom-call(f32[2,8,128]{2,1,0:T(8,128)S(1)} %get-tuple-element.12.refs_1_.info_ref, bf16[32,16,256]{2,1,0:T(8,128)(2,1)S(1)} %bitcast.12), custom_call_target="tpu_custom_call" | custom-call | tf_op jit(solution)/shard_map/select/pallas_call | solution.py:303
  (5 shorter events, 0.1 us)
Async XLA Ops:
  0.0 4.3 %collective-permute-start = (bf16[256,32]{1,0:T(8,128)(2,1)}, bf16[256,32]{1,0:T(8,128)(2,1)S(1)}, u32[]{:S(2)}, u32[]{:S(2)}) collective-permute-start(bf16[256,32]{1,0:T(8,128)(2,1)} %bitcast.15), channel_id=1, source_target_pairs={{0,16},{16,0},{1,17},{17,1},{2,18},{18,2},{3,19},{19,3},{4,20},{20... | collective-permute-start | bytes 49160 | tf_op jit(solution)/shard_map/ppermute | solution.py:324
  4.3 27.2 %collective-permute-start.1 = (bf16[28,256,256]{2,1,0:T(8,128)(2,1)}, bf16[28,256,256]{2,1,0:T(8,128)(2,1)}, u32[]{:S(2)}, u32[]{:S(2)}) collective-permute-start(bf16[28,256,256]{2,1,0:T(8,128)(2,1)} %refs_5_.1), channel_id=1, source_target_pairs={{0,16},{16,0},{1,17},{17,1},{2,18},{18,2},{3,19},{19,3},{4,20},{20... | collective-permute-start | bytes 11010056 | tf_op jit(solution)/shard_map/ppermute | solution.py:329
  38.3 3.1 %collective-permute-start.2 = (f32[256,256]{1,0:T(8,128)S(1)}, f32[256,256]{1,0:T(8,128)S(1)}, u32[]{:S(2)}, u32[]{:S(2)}) collective-permute-start(f32[256,256]{1,0:T(8,128)S(1)} %ladder.1.own_ref), channel_id=1, source_target_pairs={{0,16},{16,0},{1,17},{17,1},{2,18},{18,2},{3,19},{19,3},{4,20},{20... | collective-permute-start | bytes 786440 | tf_op jit(solution)/shard_map/ppermute | solution.py:337

commit v6 on v3

--- a/solution.py
+++ b/solution.py
@@ -6,14 +6,15 @@
 from jax.sharding import Mesh
 from jax.sharding import PartitionSpec as P
 
+
 BF16 = jnp.bfloat16
 F32 = jnp.float32
 NT = (((1,), (1,)), ((), ()))
-HEAD = 8
-HEAD_PARTS = 2
-REST_PARTS = 4
+NEAR_HEAD = 20
+FAR_HEAD = 8
 VMEM_SPEC = pl.BlockSpec(memory_space=pltpu.VMEM)
 HBM_SPEC = pl.BlockSpec(memory_space=pltpu.HBM)
+SMEM_SPEC = pl.BlockSpec(memory_space=pltpu.SMEM)
 
 
 def in_hbm(x):
@@ -31,6 +32,7 @@
 
 
 def plan_kernel(
+    near_ref,
     group_ref,
     amp_hbm,
     partner_hbm,
@@ -54,12 +56,18 @@
     sources = (partner_hbm, owner_hbm, amp_hbm, energy_hbm, virt_hbm)
     targets = (partner_ref, owner_ref, amp_ref, energy_ref, virt_ref)
     copies = [pltpu.make_async_copy(a, b, sems.at[i]) for i, (a, b) in enumerate(zip(sources, targets))]
-    part = head_ref.shape[0] // HEAD_PARTS
-    for i in range(HEAD_PARTS):
-        rows = pl.ds(i * part, part)
-        copies.append(pltpu.make_async_copy(three_hbm.at[rows], head_ref.at[rows], sems.at[len(sources) + i]))
+    first = pl.ds(0, FAR_HEAD)
+    tail = pl.ds(FAR_HEAD, head_ref.shape[0] - FAR_HEAD)
+    copies.append(pltpu.make_async_copy(three_hbm.at[first], head_ref.at[first], sems.at[5]))
+    rest = pltpu.make_async_copy(three_hbm.at[tail], head_ref.at[tail], sems.at[6])
+    near = near_ref[0] > 0
     for copy in copies:
         copy.start()
+
+    @pl.when(near)
+    def _():
+        rest.start()
+
     count = partner_ref.shape[1]
     square = (count, count)
     group = group_ref[...]
@@ -102,34 +110,38 @@
     same = jnp.where(group >= jnp.broadcast_to(leaders, wide), 1.0, 0.0)
     info_ref[0] = jnp.where(iota(wide, 0) == 2, same, energies)
     info_ref[1] = jnp.broadcast_to(found, wide).astype(F32)
-    for copy in copies[len(sources) :]:
-        copy.wait()
-
-
-def plan(amplitudes, partner, owner, pair_energy, virt_energy, three_index, group, capacity):
+    copies[5].wait()
+
+    @pl.when(near)
+    def _():
+        rest.wait()
+
+
+def plan(near, amplitudes, partner, owner, pair_energy, virt_energy, three_index, group, capacity):
     count, side, _ = amplitudes.shape
     virt = virt_energy.shape[0]
     amp = jnp.transpose(amplitudes, (1, 2, 0)).reshape(side * side, count)
     return pl.pallas_call(
         lambda *refs: plan_kernel(*refs, side=side, capacity=capacity),
-        in_specs=[VMEM_SPEC] + [HBM_SPEC] * 6,
+        in_specs=[SMEM_SPEC, VMEM_SPEC] + [HBM_SPEC] * 6,
         out_specs=[VMEM_SPEC] * 4,
         out_shape=[
             jax.ShapeDtypeStruct((count, side * side), BF16),
             jax.ShapeDtypeStruct((2, 8, 128), F32),
             jax.ShapeDtypeStruct((1, virt), F32),
-            jax.ShapeDtypeStruct((HEAD,) + three_index.shape[1:], BF16),
+            jax.ShapeDtypeStruct((NEAR_HEAD,) + three_index.shape[1:], BF16),
         ],
         scratch_shapes=[
             pltpu.VMEM((side * side, count), BF16),
             pltpu.VMEM((1, count), jnp.int32),
             pltpu.VMEM((1, count), jnp.int32),
             pltpu.VMEM((1, count), F32),
-            pltpu.SemaphoreType.DMA((5 + HEAD_PARTS,)),
+            pltpu.SemaphoreType.DMA((7,)),
         ],
         compiler_params=pltpu.CompilerParams(vmem_limit_bytes=8 << 20),
         name="plan",
     )(
+        near,
         jnp.full((8, 128), group, jnp.int32),
         in_hbm(amp),
         in_hbm(partner.reshape(1, count)),
@@ -140,80 +152,143 @@
     )
 
 
-def ladder_kernel(core_ref, info_ref, virt_ref, own_ref, other_ref, head_ref, three_hbm, keep_ref, send_ref, turned, rest_ref, sems, *, side):
-    virt = head_ref.shape[1]
-    head = head_ref.shape[0]
-    part = rest_ref.shape[0] // REST_PARTS
-    copies = []
-    for i in range(REST_PARTS):
-        source = three_hbm.at[pl.ds(head + i * part, part)]
-        copies.append(pltpu.make_async_copy(source, rest_ref.at[pl.ds(i * part, part)], sems.at[i]))
-        copies[-1].start()
-    half_lanes = virt // 2
-    per_vector = half_lanes // side
-    first_core = jnp.broadcast_to(core_ref[:1, :] == 0, (side, half_lanes))
-
-    def piece(slot, z, core, half):
-        rows = pl.ds(z * side, side)
-        lanes = pl.ds(half * half_lanes, half_lanes)
-        own = own_ref[slot, rows, lanes].astype(F32)
-        other = other_ref[slot, rows, lanes].astype(F32)
-        return jnp.where(first_core, own, other) if core == 0 else jnp.where(first_core, other, own)
-
-    order = [(slot, half, high) for slot in range(2) for half in range(2) for high in range(2)]
-    vectors = []
-    for low in range(per_vector):
-        z_low, core = low // 2, low % 2
-        vectors.append(
-            jnp.concatenate(
-                [piece(slot, high * (per_vector // 2) + z_low, core, half) for slot, half, high in order], axis=0
-            )
-        )
+def half_columns(tiles_ref, turned, even, side, virt):
+    lanes_of = virt // 2
+    groups = lanes_of // side
+    low = [i // 2 + (groups // 2) * (i % 2) for i in range(groups)]
+    high = [low[(i - 1) % groups] for i in range(groups)]
+    order = [(slot, half) for slot in range(2) for half in range(2)]
+
+    def piece(slot, half, i):
+        lanes = pl.ds(half * lanes_of, lanes_of)
+        a = tiles_ref[slot, pl.ds(low[i] * side, side), lanes]
+        b = tiles_ref[slot, pl.ds(high[i] * side, side), lanes]
+        return jnp.where(even, a, b)
+
+    vectors = [jnp.concatenate([piece(slot, half, i) for slot, half in order], axis=0) for i in range(groups)]
     lane_group = iota(vectors[0].shape, 1) // side
     step = 1
-    while step < per_vector:
+    while step < groups:
         keep = (lane_group & step) == 0
         shift = step * side
-        for i in range(per_vector):
+        for i in range(groups):
             if i & step:
                 continue
             j = i | step
             a, b = vectors[i], vectors[j]
             vectors[i] = jnp.where(keep, a, pltpu.roll(b, shift, 1))
-            vectors[j] = jnp.where(keep, pltpu.roll(a, half_lanes - shift, 1), b)
+            vectors[j] = jnp.where(keep, pltpu.roll(a, lanes_of - shift, 1), b)
         step *= 2
-    for s_low in range(per_vector):
-        vector = vectors[s_low].astype(BF16)
-        for k, (slot, half, high) in enumerate(order):
-            rows = pl.ds((half * per_vector + s_low) * side, side)
-            lanes = pl.ds(slot * virt + high * half_lanes, half_lanes)
-            turned[rows, lanes] = vector[k * side : (k + 1) * side]
-    amp_t = jnp.dot(swap_matrix(side), turned[...], preferred_element_type=F32).astype(BF16)
-
-    totals = [jnp.zeros((virt, virt), F32)] * 2
-    for i in range(REST_PARTS + 1):
-        if i == 0:
-            block_ref = head_ref
-        else:
-            copies[i - 1].wait()
-            block_ref = rest_ref.at[pl.ds((i - 1) * part, part)]
-        count = block_ref.shape[0]
-        rows = block_ref[...].reshape(count * virt, virt)
-        half = jnp.dot(rows, amp_t, preferred_element_type=F32).astype(BF16)
+    for i in range(groups):
+        for k, (slot, half) in enumerate(order):
+            rows = pl.ds((half * groups + i) * side, side)
+            turned[rows, pl.ds(slot * lanes_of, lanes_of)] = vectors[i][k * side : (k + 1) * side]
+    return jnp.dot(swap_matrix(side), turned[...], preferred_element_type=F32).astype(BF16)
+
+
+def half_ladder(total, block, amp_t, plain, side):
+    count, virt, _ = block.shape
+    lanes_of = virt // 2
+    product = jnp.dot(block[...].reshape(count * virt, virt), amp_t, preferred_element_type=F32).astype(BF16)
+
+    def gathered(q):
+        return jnp.where(plain, block[q, :, :lanes_of], pltpu.roll(block[q, :, lanes_of:], side, 1))
+
+    for q in range(0, count, 2):
+        left = []
         for slot in range(2):
-            for q in range(count):
-                totals[slot] = totals[slot] + lax.dot_general(
-                    half[q * virt : (q + 1) * virt, slot * virt : (slot + 1) * virt],
-                    block_ref[q],
-                    NT,
-                    preferred_element_type=F32,
+            lanes = slice(slot * lanes_of, (slot + 1) * lanes_of)
+            left.append(
+                jnp.concatenate(
+                    [product[q * virt : (q + 1) * virt, lanes], product[(q + 1) * virt : (q + 2) * virt, lanes]], axis=1
                 )
+            )
+        right = jnp.concatenate([gathered(q), gathered(q + 1)], axis=1)
+        total += lax.dot_general(jnp.concatenate(left, axis=0), right, NT, preferred_element_type=F32)
+    return total
+
+
+def masks(core_ref, which, side, virt):
+    lanes_of = virt // 2
+    parity = jnp.bitwise_xor(core_ref[:1, :], which)
+    even = jnp.broadcast_to(parity == 0, (side, lanes_of))
+    shape = (virt, lanes_of)
+    plain = (iota(shape, 1) // side) % 2 == jnp.broadcast_to(parity, shape)
+    return even, plain
+
+
+def own_kernel(near_ref, core_ref, tiles_ref, head_ref, three_hbm, total_ref, rest_ref, turned, sems, *, side):
+    near = near_ref[0] > 0
+    far_rest, virt, _ = rest_ref.shape
+    skipped = NEAR_HEAD - FAR_HEAD
+    tail = pl.ds(skipped, far_rest - skipped)
+    middle = pltpu.make_async_copy(three_hbm.at[pl.ds(FAR_HEAD, skipped)], rest_ref.at[pl.ds(0, skipped)], sems.at[0])
+    last = pltpu.make_async_copy(three_hbm.at[pl.ds(NEAR_HEAD, far_rest - skipped)], rest_ref.at[tail], sems.at[1])
+
+    @pl.when(jnp.logical_not(near))
+    def _():
+        middle.start()
+
+    last.start()
+    even, plain = masks(core_ref, 0, side, virt)
+    amp_t = half_columns(tiles_ref, turned, even, side, virt)
+    zero = jnp.zeros((2 * virt, virt), F32)
+
+    @pl.when(near)
+    def _():
+        total = half_ladder(zero, head_ref, amp_t, plain, side)
+        last.wait()
+        total_ref[...] = half_ladder(total, rest_ref.at[tail], amp_t, plain, side)
+
+    @pl.when(jnp.logical_not(near))
+    def _():
+        total = half_ladder(zero, head_ref.at[pl.ds(0, FAR_HEAD)], amp_t, plain, side)
+        middle.wait()
+        last.wait()
+        total_ref[...] = half_ladder(total, rest_ref, amp_t, plain, side)
+
+
+def own_half(near, core, tiles, head, three_index, side):
+    naux, virt, _ = three_index.shape
+    return pl.pallas_call(
+        lambda *refs: own_kernel(*refs, side=side),
+        in_specs=[SMEM_SPEC] + [VMEM_SPEC] * 3 + [HBM_SPEC],
+        out_specs=[VMEM_SPEC] * 2,
+        out_shape=[
+            jax.ShapeDtypeStruct((2 * virt, virt), F32),
+            jax.ShapeDtypeStruct((naux - FAR_HEAD, virt, virt), BF16),
+        ],
+        scratch_shapes=[pltpu.VMEM((virt, virt), BF16), pltpu.SemaphoreType.DMA((2,))],
+        compiler_params=pltpu.CompilerParams(vmem_limit_bytes=24 << 20),
+        cost_estimate=pl.CostEstimate(flops=1 << 30, bytes_accessed=4 << 20, transcendentals=0),
+        name="own",
+    )(near, jnp.full((8, 128), core, jnp.int32), tiles, head, in_hbm(three_index))
+
+
+def other_kernel(
+    near_ref, core_ref, info_ref, virt_ref, tiles_ref, head_ref, rest_ref, total_ref, keep_ref, send_ref, turned, sum_ref, *, side
+):
+    near = near_ref[0] > 0
+    far_rest, virt, _ = rest_ref.shape
+    skipped = NEAR_HEAD - FAR_HEAD
+    even, plain = masks(core_ref, 1, side, virt)
+    amp_t = half_columns(tiles_ref, turned, even, side, virt)
+
+    @pl.when(near)
+    def _():
+        total = half_ladder(total_ref[...], head_ref, amp_t, plain, side)
+        sum_ref[...] = half_ladder(total, rest_ref.at[pl.ds(skipped, far_rest - skipped)], amp_t, plain, side)
+
+    @pl.when(jnp.logical_not(near))
+    def _():
+        total = half_ladder(total_ref[...], head_ref.at[pl.ds(0, FAR_HEAD)], amp_t, plain, side)
+        sum_ref[...] = half_ladder(total, rest_ref, amp_t, plain, side)
 
     rows_of = jnp.broadcast_to(virt_ref[...], (virt, virt))
     sums = rows_of + rows_of.T
     info = info_ref[0]
-    first = totals[0] / (sums - info[0:1, 0:1])
-    second = totals[1] / (sums - info[1:2, 0:1])
+    first = sum_ref[:virt, :] / (sums - info[0:1, 0:1])
+    second = sum_ref[virt:, :] / (sums - info[1:2, 0:1])
     same = jnp.broadcast_to(info[2:3, 0:1] > 0.5, (virt, virt))
     blocks = (first.T + jnp.where(same, first, second), second.T + jnp.where(same, second, first))
     on_first = jnp.broadcast_to(core_ref[:1, :1] == 0, (virt, virt))
@@ -221,29 +296,17 @@
     send_ref[...] = jnp.where(on_first, blocks[1], blocks[0])
 
 
-def ladder(core, info, virt_row, own, other, head, three_index, side):
-    naux, virt, _ = three_index.shape
-    return pl.pallas_call(
-        lambda *refs: ladder_kernel(*refs, side=side),
-        in_specs=[VMEM_SPEC] * 6 + [HBM_SPEC],
+def other_half(near, core, info, virt_row, tiles, head, rest, total, side):
+    virt = head.shape[1]
+    return pl.pallas_call(
+        lambda *refs: other_kernel(*refs, side=side),
+        in_specs=[SMEM_SPEC] + [VMEM_SPEC] * 7,
         out_specs=[VMEM_SPEC] * 2,
         out_shape=[jax.ShapeDtypeStruct((virt, virt), F32)] * 2,
-        scratch_shapes=[
-            pltpu.VMEM((virt, 2 * virt), BF16),
-            pltpu.VMEM((naux - HEAD, virt, virt), BF16),
-            pltpu.SemaphoreType.DMA((REST_PARTS,)),
-        ],
-        compiler_params=pltpu.CompilerParams(vmem_limit_bytes=40 << 20),
-        name="ladder",
-    )(
-        jnp.full((8, 128), core, jnp.int32),
-        info,
-        virt_row,
-        own,
-        other,
-        head,
-        in_hbm(three_index),
-    )
+        scratch_shapes=[pltpu.VMEM((virt, virt), BF16), pltpu.VMEM((2 * virt, virt), F32)],
+        compiler_params=pltpu.CompilerParams(vmem_limit_bytes=24 << 20),
+        name="other",
+    )(near, jnp.full((8, 128), core, jnp.int32), info, virt_row, tiles, head, rest, total)
 
 
 def merge_kernel(kept_ref, came_ref, out_ref):
@@ -311,8 +374,9 @@
     pairs_all, side, _ = amplitudes.shape
     virt = three_index.shape[1]
     capacity = 2 * (pairs_all // groups)
+    near = (lax.axis_index("z") < depth // 2).astype(jnp.int32).reshape(1)
     tiles, info, virt_row, head = plan(
-        amplitudes, partner, owner, pair_energy, virt_energy, three_index, lax.axis_index("pairs"), capacity
+        near, amplitudes, partner, owner, pair_energy, virt_energy, three_index, lax.axis_index("pairs"), capacity
     )
     outgoing = jnp.broadcast_to(
         tiles.reshape(1, groups, 2, side * side), (depth, groups, 2, side * side)
@@ -320,7 +384,8 @@
     arrived = lax.all_to_all(outgoing, ("z", "pairs"), split_axis=0, concat_axis=0, tiled=True)
     own = jnp.transpose(arrived, (1, 0, 2))
     other = lax.ppermute(own, "core", swap)
-    keep, send = ladder(core, info, virt_row, own, other, head, three_index, side)
+    total, rest = own_half(near, core, own, head, three_index, side)
+    keep, send = other_half(near, core, info, virt_row, other, head, rest, total, side)
     partial = merge(keep, lax.ppermute(send, "core", swap), aux)
     shares = lax.all_to_all(partial, aux_axes, split_axis=0, concat_axis=0, tiled=True)
     spread = gather(shares, groups)

time: 62.5 us -> 62.8 us (level)
  Pallas kernels: 6.91 us -> 8.84 us
  blocking collectives: 50.4 us -> 49.7 us
  waiting for transfers between devices: 2.16 us -> 1.51 us
    pallas_call x1 -> x2, Pallas kernels: 4.81 us -> 6.21 us  [the longest x1 3.15 us: other_half(): pl.pallas_call(lambda *refs: other_kernel(*refs, side=side), in_specs=[SM...]
    ppermute x1, waiting for transfers between devices: 0.99 us -> 0.01 us  [per_device(): other = lax.ppermute(own, 'core', swap)]
  transfers between devices with their start and end apart: 2 -> 2, of which waited for: 2 -> 1; matrix products, arithmetic and copies ran while one was open for 0% -> 0% of each run, Pallas kernels for 0% -> 5%
where the time goes in v6:
time: 62.8 us; the launch traced here: 62.5 us
  blocking collectives  49.7 us (79%)
  Pallas kernels  8.84 us (14%)
  starting transfers between devices  2.3 us (4%)
  waiting for transfers between devices  1.51 us (2%)
    all_to_all x1, blocking collectives, per_device(): lax.all_to_all(outgoing, ('z', 'pairs'), split_axis=0, concat_axis=0, til...  26.9 us
    all_to_all x1, blocking collectives, per_device(): lax.all_to_all(partial, aux_axes, split_axis=0, concat_axis=0, tiled=True)  11.7 us
    all_to_all x1, blocking collectives, per_device(): lax.all_to_all(spread, 'pairs', split_axis=0, concat_axis=0, tiled=True)  11.1 us
    pallas_call x1, Pallas kernels, other_half(): pl.pallas_call(lambda *refs: other_kernel(*refs, side=side), in_specs=[SM...  3.15 us
    pallas_call x1, Pallas kernels, own_half(): pl.pallas_call(lambda *refs: own_kernel(*refs, side=side), in_specs=[SMEM...  3.06 us
    ppermute x1, starting transfers between devices, per_device(): other = lax.ppermute(own, 'core', swap)  2.19 us
    pallas_call x1, Pallas kernels, plan(): pl.pallas_call(lambda *refs: plan_kernel(*refs, side=side, capacity=capac...  1.89 us
    ppermute x1, waiting for transfers between devices, per_device(): partial = merge(keep, lax.ppermute(send, 'core', swap), aux)  1.51 us
  transfers between devices with their start and end apart: 2, of which 1 were waited for; matrix products, arithmetic and copies ran while one was open for 0% of the time, Pallas kernels for 5%

profile of v6, /device:TPU:1, one launch (start us, length us, event | category | flops | bytes accessed | tf_op | source)
XLA Modules:
  0.0 62.5 jit_solution(5845496668100431985)
XLA Ops:
  0.0 1.9 %plan.1 = (bf16[32,256]{1,0:T(8,128)(2,1)S(1)}, f32[2,8,128]{2,1,0:T(8,128)S(1)}, f32[1,256]{1,0:T(1,128)S(1)}, bf16[20,256,256]{2,1,0:T(8,128)(2,1)S(1)}) custom-call(s32[1]{0:T(128)} %bitcast.refs_0_, s32[8,128]{1,0:T(8,128)S(1)} %broadcast_in_dim.14.refs_1_, bf16[256,32]{1,0:T(8,128)(2,1)} %bitcast.17, s32[1,32]{1,0:T(1,128)} %bitcast.19, ...), custom_call_target="tpu_custom_call" | custom-call | tf_op jit(solution)/shard_map/plan/pallas_call | solution.py:124
  1.9 0.1 broadcast_in_dim.17
  2.0 26.9 %all_to_all.15 = bf16[128,2,256]{2,1,0:T(2,128)(2,1)S(1)} all-to-all(bf16[128,2,256]{2,1,0:T(2,128)(2,1)S(1)} %bitcast.16), channel_id=1, replica_groups=mesh['z'=8,'core'=2,'pairs'=16] {'z','pairs'}, dimensions={0} | all-to-all | bytes 262144 | tf_op jit(solution)/shard_map/all_to_all | solution.py:384
  28.9 2.2 %collective-permute-start = (bf16[2,128,256]{2,1,0:T(8,128)(2,1)S(1)}, bf16[2,128,256]{2,1,0:T(8,128)(2,1)S(1)}, u32[]{:S(2)}, u32[]{:S(2)}) collective-permute-start(bf16[2,128,256]{2,1,0:T(8,128)(2,1)S(1)} %bitcast.14), channel_id=1, source_target_pairs={{0,16},{16,0},{1,17},{17,1},{2,18},{18,2},{3,19},{19,3},{4,20},{20... | collective-permute-start | bytes 393224 | tf_op jit(solution)/shard_map/ppermute | solution.py:386
  31.1 3.1 %own.1 = (f32[512,256]{1,0:T(8,128)S(1)}, bf16[20,256,256]{2,1,0:T(8,128)(2,1)S(1)}) custom-call(s32[1]{0:T(128)} %bitcast.refs_0_, s32[8,128]{1,0:T(8,128)S(1)} %broadcast_in_dim.15.refs_1_, bf16[2,128,256]{2,1,0:T(8,128)(2,1)S(1)} %bitcast.15, bf16[20,256,256]{2,1,0:T(8,128)(2,1)S(1)} %get-tuple-element.16.refs_3_.refs_5_, bf16[28,256,256]{2,1,0:T(8,128)(2,1)} %refs_4_.1), custom_call_target="tpu_custom_call" | custom-call | flops 1073741824 | bytes 4194304 | tf_op jit(solution)/shard_map/own/pallas_call | solution.py:253
  34.2 0.0 collective-permute-done.refs_4_
  34.2 3.1 %other.1 = (f32[256,256]{1,0:T(8,128)S(1)}, f32[256,256]{1,0:T(8,128)S(1)}) custom-call(s32[1]{0:T(128)} %bitcast.refs_0_, s32[8,128]{1,0:T(8,128)S(1)} %broadcast_in_dim.15.refs_1_, f32[2,8,128]{2,1,0:T(8,128)S(1)} %get-tuple-element.13.refs_2_.info_ref, f32[1,256]{1,0:T(1,128)S(1)} %get-tuple-element.14.refs_3_, ...), custom_call_target="tpu_custom_call" | custom-call | tf_op jit(solution)/shard_map/other/pallas_call | solution.py:301
  37.3 0.1 collective-permute-start.1
  37.4 1.5 %collective-permute-done.1.came_ref = f32[256,256]{1,0:T(8,128)S(1)} collective-permute-done((f32[256,256]{1,0:T(8,128)S(1)}, f32[256,256]{1,0:T(8,128)S(1)}, u32[]{:S(2)}, u32[]{:S(2)}) %collective-permute-start.1) | collective-permute-done | bytes 262176 | tf_op jit(solution)/shard_map/ppermute | solution.py:389
  39.0 11.7 %all_to_all.16.shares_ref = bf16[16,16,256]{2,1,0:T(8,128)(2,1)S(1)} all-to-all(bf16[16,16,256]{2,1,0:T(8,128)(2,1)S(1)} %merge.1), channel_id=1, replica_groups=mesh['z'=8,'core'=2,'pairs'=16] {'z','core'}, dimensions={0} | all-to-all | bytes 262144 | tf_op jit(solution)/shard_map/all_to_all | solution.py:390
  50.7 11.1 %all_to_all.17 = bf16[16,2,16,256]{3,2,1,0:T(8,128)(2,1)S(1)} all-to-all(bf16[16,2,16,256]{3,2,1,0:T(8,128)(2,1)S(1)} %gather.1), channel_id=1, replica_groups=mesh['z'=8,'core'=2,'pairs'=16] {'pairs'}, dimensions={0} | all-to-all | bytes 524288 | tf_op jit(solution)/shard_map/all_to_all | solution.py:392
  61.9 0.7 %select.1 = f32[4,16,256]{2,1,0:T(8,128)} custom-call(f32[2,8,128]{2,1,0:T(8,128)S(1)} %get-tuple-element.13.refs_2_.info_ref, bf16[32,16,256]{2,1,0:T(8,128)(2,1)S(1)} %bitcast.13), custom_call_target="tpu_custom_call" | custom-call | tf_op jit(solution)/shard_map/select/pallas_call | solution.py:357
  (6 shorter events, 0.1 us)
Async XLA Ops:
  28.9 5.3 %collective-permute-start = (bf16[2,128,256]{2,1,0:T(8,128)(2,1)S(1)}, bf16[2,128,256]{2,1,0:T(8,128)(2,1)S(1)}, u32[]{:S(2)}, u32[]{:S(2)}) collective-permute-start(bf16[2,128,256]{2,1,0:T(8,128)(2,1)S(1)} %bitcast.14), channel_id=1, source_target_pairs={{0,16},{16,0},{1,17},{17,1},{2,18},{18,2},{3,19},{19,3},{4,20},{20... | collective-permute-start | bytes 393224 | tf_op jit(solution)/shard_map/ppermute | solution.py:386
  37.3 1.6 %collective-permute-start.1 = (f32[256,256]{1,0:T(8,128)S(1)}, f32[256,256]{1,0:T(8,128)S(1)}, u32[]{:S(2)}, u32[]{:S(2)}) collective-permute-start(f32[256,256]{1,0:T(8,128)S(1)} %get-tuple-element.20), channel_id=1, source_target_pairs={{0,16},{16,0},{1,17},{17,1},{2,18},{18,2},{3,19},{19,3},{4,20},{20... | collective-permute-start | bytes 786440 | tf_op jit(solution)/shard_map/ppermute | solution.py:389
